TPU v7x, 128 devices: a whole 4x4x4 slice. The times are simulated.
128 devices in a mesh: gx: 16 (over z, y), gy: 8 (over x, core).
Axes of the slice: x: 4, y: 4, z: 4, core: 2. Of those that a mesh axis runs over, the one named last changes fastest.
Arguments:
- head_old: float32 [10, 256, 4096], P(None, 'gx', 'gy'), may hold values from -4 to 4
- soil_type: int32 [10, 256, 4096], P(None, 'gx', 'gy'), may hold values from 0 to 11
- soil_table: float32 [3, 12], replicated, may hold values from 0.2 to 3, as said below
- forcing: float32 [4, 256, 4096], P(None, 'gx', 'gy'), may hold values from 0 to 2, as said below
- canopy: float32 [13, 1048576], P(None, ('gx', 'gy')), may hold values from 0.05 to 6, as said below
- column_slot: int32 [256, 4096], P('gx', 'gy'), may hold values from -1 to 8191, as said below
Outputs:
- head_new: float32 [10, 256, 4096], P(None, 'gx', 'gy')
- surface_flux: float32 [2, 256, 4096], P(None, 'gx', 'gy')
Inputs may be any that keep to these rules, and one draw needn't show every extreme that they name: `soil_table`: Rows: conductivity 0.2 to 2, steepness 0.5 to 3, capacity 0.2 to 0.5. `forcing`: Rows: sunlight 0.5 to 2, air temperature 0.8 to 1.2, humidity 0 to 0.5, rainfall 0.1 to 2. `canopy`: Rows: leaf area 0.5 to 6, albedo 0.1 to 0.3, resistance 0.2 to 5, root weights 0.05 to 1. `column_slot`: the land cells of one device's tile name distinct values; the value v sends the column to the device of index v // 64 along gx+gy into slot v % 64; in every draw some device uses every value.
All inputs are finite; a program needn't handle non-finite values.
Results may differ from a plain program's by a relative error of at most 0.00029.
Values sent between devices are 32-bit elements; how exact they have to be, the bound alone decides.
A program may use at most 64 MiB of HBM per device.

v0:
```python
import jax
import jax.numpy as jnp
from jax import lax
from jax.sharding import PartitionSpec as P

NEWTON = 2
KRYLOV = 3


storage_weight = 4.0
norm_epsilon = 1e-06


def padded_2(x, sides, width):
    for axis, dim in sides:
        size, length = (lax.axis_size(axis), x.shape[dim])
        up = [(i, (i + 1) % size) for i in range(size - 1)]
        down = [(j, i) for i, j in up]
        last = lax.slice_in_dim(x, length - width, length, axis=dim)
        initial = lax.slice_in_dim(x, 0, width, axis=dim)
        before = lax.ppermute(last, axis, up)
        after = lax.ppermute(initial, axis, down)
        x = jnp.concatenate([before, x, after], axis=dim)
    return x


def soil_fields(soil_type, soil_table):
    conduct = jnp.zeros(soil_type.shape, jnp.float32)
    steep = jnp.zeros(soil_type.shape, jnp.float32)
    capacity = jnp.zeros(soil_type.shape, jnp.float32)
    for kind in range(soil_table.shape[1]):
        match = soil_type == kind
        conduct = jnp.where(match, soil_table[0, kind], conduct)
        steep = jnp.where(match, soil_table[1, kind], steep)
        capacity = jnp.where(match, soil_table[2, kind], capacity)
    return jnp.stack([conduct, steep, capacity])


def balance(padded, params, theta_old, source):
    sat = jax.nn.sigmoid(params[1] * padded)
    conduct = params[0] * (0.1 + 0.9 * sat * sat)
    head = padded[:, 1:-1, 1:-1]
    inner = conduct[:, 1:-1, 1:-1]
    theta = params[2][:, 1:-1, 1:-1] * sat[:, 1:-1, 1:-1]
    lateral = jnp.zeros_like(head)
    for near_head, near_cond in (
        (padded[:, 2:, 1:-1], conduct[:, 2:, 1:-1]),
        (padded[:, :-2, 1:-1], conduct[:, :-2, 1:-1]),
        (padded[:, 1:-1, 2:], conduct[:, 1:-1, 2:]),
        (padded[:, 1:-1, :-2], conduct[:, 1:-1, :-2]),
    ):
        lateral = lateral + 0.5 * (inner + near_cond) * (head - near_head)
    face = 0.5 * (inner[:-1] + inner[1:]) * (head[:-1] - head[1:] + 1.0)
    below = jnp.concatenate([face, inner[-1:]], axis=0)
    above = jnp.concatenate([jnp.zeros_like(head[:1]), face], axis=0)
    return storage_weight * (theta - theta_old) + lateral + below - above - source


def land_column(wet, ks_top, forcing, records):
    sunlight, air_temp, humidity, rainfall = (forcing[0], forcing[1], forcing[2], forcing[3])
    leaf_area, albedo, resist = (records[0], records[1], records[2])
    roots = records[3:]
    uptake = roots * wet
    total = jnp.sum(uptake, axis=0)
    wetness = total / jnp.sum(roots, axis=0)
    conductance = wetness * leaf_area / (leaf_area + resist)
    exchange_coef = 0.5 + 0.3 * leaf_area
    radiation = (1.0 - albedo) * sunlight + 0.3
    surface = air_temp
    for sweep_index in range(2):
        vapour = 0.5 * jnp.exp(2.0 * (surface - air_temp))
        square = surface * surface
        excess = (
            radiation
            - 0.3 * square * square
            - exchange_coef * (surface - air_temp)
            - conductance * (vapour - humidity)
        )
        slope = -1.2 * square * surface - exchange_coef - 2.0 * conductance * vapour
        surface = surface - excess / slope
    vapour = 0.5 * jnp.exp(2.0 * (surface - air_temp))
    evaporation = conductance * (vapour - humidity)
    infiltration = rainfall * ks_top / (rainfall + ks_top)
    sink = evaporation * uptake / total
    return (sink, evaporation, infiltration)


def surface_terms(land, sink, evaporation, infiltration):
    source = jnp.where(land, -sink, 0.0)
    source = source.at[0].add(jnp.where(land, infiltration, 0.0))
    flux = jnp.stack([jnp.where(land, evaporation, 0.0), jnp.where(land, infiltration, 0.0)])
    return (source, flux)


def small_solve(hessen, initial_norm):
    gram = jnp.dot(hessen.T, hessen, precision=lax.Precision.HIGHEST)
    target = hessen[0] * initial_norm
    factor = jnp.linalg.cholesky(gram)
    size = gram.shape[0]
    forward = []
    for row in range(size):
        value = target[row]
        for other in range(row):
            value = value - factor[row, other] * forward[other]
        forward.append(value / factor[row, row])
    backward = [None] * size
    for row in reversed(range(size)):
        value = forward[row]
        for other in range(row + 1, size):
            value = value - factor[other, row] * backward[other]
        backward[row] = value / factor[row, row]
    return jnp.stack(backward)


def shards(head_old, soil_type, soil_table, forcing, canopy, column_slot):
    layers, rows_x, rows_y = head_old.shape
    params = soil_fields(soil_type, soil_table)
    wet = jax.nn.sigmoid(params[1] * head_old)
    theta_old = params[2] * wet
    land = column_slot >= 0
    flat_slot = jnp.maximum(column_slot, 0).reshape(-1)
    outgoing = jnp.concatenate(
        [wet.reshape(layers, -1), params[0, 0].reshape(1, -1), forcing.reshape(4, -1)], axis=0
    )
    target = jnp.where(land, column_slot, canopy.shape[1]).reshape(-1)
    buffer = (
        jnp.zeros((outgoing.shape[0], canopy.shape[1]), jnp.float32)
        .at[:, target]
        .set(outgoing, mode="drop")
    )
    arrived = lax.all_to_all(buffer, ("gx", "gy"), split_axis=1, concat_axis=1, tiled=True)
    sink, evaporation, infiltration = land_column(
        arrived[:layers], arrived[layers], arrived[layers + 1 :], canopy
    )
    results = jnp.concatenate([sink, evaporation[None], infiltration[None]], axis=0)
    returned = lax.all_to_all(results, ("gx", "gy"), split_axis=1, concat_axis=1, tiled=True)
    local = jnp.take(returned, flat_slot, axis=1).reshape(layers + 2, rows_x, rows_y)
    sink, evaporation, infiltration = (local[:layers], local[layers], local[layers + 1])
    source, surface_flux = surface_terms(land, sink, evaporation, infiltration)
    padded_params = padded_2(params, (("gx", 2), ("gy", 3)), 1)
    head = head_old
    padded = head_old
    for newton_step in range(NEWTON):
        padded = padded_2(head, (("gx", 1), ("gy", 2)), 1)

        def residual_of(field):
            return balance(field, padded_params, theta_old, source)

        residual_now = residual_of(padded)
        initial_norm = jnp.sqrt(
            lax.psum(jnp.sum(residual_now * residual_now), ("gx", "gy")) + norm_epsilon
        )
        basis = [residual_now / initial_norm]
        rims = []
        hessen = jnp.zeros((KRYLOV + 1, KRYLOV), jnp.float32)
        for krylov_step in range(KRYLOV):
            rim = padded_2(basis[krylov_step], (("gx", 1), ("gy", 2)), 1)
            rims.append(rim)
            direction = jax.jvp(residual_of, (padded,), (rim,))[1]
            for index, earlier in enumerate(basis):
                product = lax.psum(jnp.sum(direction * earlier), ("gx", "gy"))
                direction = direction - product * earlier
                hessen = hessen.at[index, krylov_step].set(product)
            length = jnp.sqrt(lax.psum(jnp.sum(direction * direction), ("gx", "gy")) + norm_epsilon)
            hessen = hessen.at[krylov_step + 1, krylov_step].set(length)
            if krylov_step + 1 < KRYLOV:
                basis.append(direction / length)
        weights = small_solve(hessen, initial_norm)
        for index, earlier in enumerate(basis):
            head = head - weights[index] * earlier
    return (head, surface_flux)


def solution(mesh):
    return jax.shard_map(
        shards,
        mesh=mesh,
        in_specs=(
            P(None, "gx", "gy"),
            P(None, "gx", "gy"),
            P(),
            P(None, "gx", "gy"),
            P(None, ("gx", "gy")),
            P("gx", "gy"),
        ),
        out_specs=(P(None, "gx", "gy"), P(None, "gx", "gy")),
        check_vma=False,
    )
```

profile of v0, /device:TPU:1, one launch (start us, length us, event | category | flops | bytes accessed | tf_op | source)
XLA Modules:
  0.0 1750.0 jit_solution(17355211472758803991)
XLA Ops:
  4.8 9.3 add_divide_fusion
  14.1 7.7 select_bitcast_fusion.1
  25.8 23.0 %scatter_custom_fusion = f32[15,8192]{0,1:T(8,128)} fusion(s32[8192]{0:T(1024)S(1)} %bitcast.213, f32[8192,15]{1,0:T(8,128)} %copy.25, f32[]{:T(128)} %constant.506.clone.1), kind=kCustom, calls=%fused_computation.6 | custom fusion | bytes 492032 | tf_op jit(solution)/shard_map/scatter | solution.py:129
  53.5 11.9 all-to-all-start
  65.4 7.7 select_select_fusion
  132.7 13.0 all-to-all-start.1
  146.8 10.6 all-to-all-done.1
  165.0 29.9 %gather_fusion = f32[8192,12]{1,0:T(8,128)} fusion(f32[12,8192]{0,1:T(8,128)} %bitcast.186, s32[8192]{0:T(1024)S(1)} %broadcast_clamp_fusion), kind=kCustom, calls=%fused_computation | custom fusion | bytes 819200 | tf_op jit(solution)/shard_map/jit(_take)/gather | solution.py:137
  194.9 6.2 select_bitcast_fusion
  212.8 5.2 multiply_reduce_fusion.19
  217.9 62.9 %psum.140 = f32[]{:T(128)} all-reduce(f32[]{:T(128)} %get-tuple-element.281), channel_id=1, replica_groups=mesh['gx'=16,'gy'=8] {'gx','gy'}, use_global_device_ids=true, to_apply=%region_4.5 | all-reduce | flops 1 | bytes 8 | tf_op jit(solution)/shard_map/psum | solution.py:151
  305.2 66.4 %psum.141 = f32[]{:T(128)} all-reduce(f32[]{:T(128)} %get-tuple-element.277), channel_id=1, replica_groups=mesh['gx'=16,'gy'=8] {'gx','gy'}, use_global_device_ids=true, to_apply=%region_6.7 | all-reduce | flops 1 | bytes 8 | tf_op jit(solution)/shard_map/psum | solution.py:161
  374.0 62.7 %psum.142 = f32[]{:T(128)} all-reduce(f32[]{:T(128)} %multiply_reduce_fusion.17), channel_id=1, replica_groups=mesh['gx'=16,'gy'=8] {'gx','gy'}, use_global_device_ids=true, to_apply=%region_8.9 | all-reduce | flops 1 | bytes 8 | tf_op jit(solution)/shard_map/psum | solution.py:164
  463.2 66.0 %psum.143 = f32[]{:T(128)} all-reduce(f32[]{:T(128)} %get-tuple-element.273), channel_id=1, replica_groups=mesh['gx'=16,'gy'=8] {'gx','gy'}, use_global_device_ids=true, to_apply=%region_10.11 | all-reduce | flops 1 | bytes 8 | tf_op jit(solution)/shard_map/psum | solution.py:161
  531.6 63.6 %psum.144 = f32[]{:T(128)} all-reduce(f32[]{:T(128)} %multiply_reduce_fusion.15), channel_id=1, replica_groups=mesh['gx'=16,'gy'=8] {'gx','gy'}, use_global_device_ids=true, to_apply=%region_12.13 | all-reduce | flops 1 | bytes 8 | tf_op jit(solution)/shard_map/psum | solution.py:161
  598.2 62.6 %psum.145 = f32[]{:T(128)} all-reduce(f32[]{:T(128)} %get-tuple-element.271), channel_id=1, replica_groups=mesh['gx'=16,'gy'=8] {'gx','gy'}, use_global_device_ids=true, to_apply=%region_14.15 | all-reduce | flops 1 | bytes 8 | tf_op jit(solution)/shard_map/psum | solution.py:164
  687.2 66.5 %psum.146 = f32[]{:T(128)} all-reduce(f32[]{:T(128)} %get-tuple-element.267), channel_id=1, replica_groups=mesh['gx'=16,'gy'=8] {'gx','gy'}, use_global_device_ids=true, to_apply=%region_17.18 | all-reduce | flops 1 | bytes 8 | tf_op jit(solution)/shard_map/psum | solution.py:161
  756.1 63.1 %psum.147 = f32[]{:T(128)} all-reduce(f32[]{:T(128)} %multiply_reduce_fusion.12), channel_id=1, replica_groups=mesh['gx'=16,'gy'=8] {'gx','gy'}, use_global_device_ids=true, to_apply=%region_19.20 | all-reduce | flops 1 | bytes 8 | tf_op jit(solution)/shard_map/psum | solution.py:161
  822.1 63.5 %psum.148 = f32[]{:T(128)} all-reduce(f32[]{:T(128)} %get-tuple-element.265), channel_id=1, replica_groups=mesh['gx'=16,'gy'=8] {'gx','gy'}, use_global_device_ids=true, to_apply=%region_21.22 | all-reduce | flops 1 | bytes 8 | tf_op jit(solution)/shard_map/psum | solution.py:161
  888.9 62.7 %psum.149 = f32[]{:T(128)} all-reduce(f32[]{:T(128)} %multiply_reduce_fusion.10), channel_id=1, replica_groups=mesh['gx'=16,'gy'=8] {'gx','gy'}, use_global_device_ids=true, to_apply=%region_23.24 | all-reduce | flops 1 | bytes 8 | tf_op jit(solution)/shard_map/psum | solution.py:164
  992.3 66.2 %psum.150 = f32[]{:T(128)} all-reduce(f32[]{:T(128)} %get-tuple-element.254), channel_id=1, replica_groups=mesh['gx'=16,'gy'=8] {'gx','gy'}, use_global_device_ids=true, to_apply=%region_27.29 | all-reduce | flops 1 | bytes 8 | tf_op jit(solution)/shard_map/psum | solution.py:151
  1082.7 66.0 %psum.151 = f32[]{:T(128)} all-reduce(f32[]{:T(128)} %get-tuple-element.250), channel_id=1, replica_groups=mesh['gx'=16,'gy'=8] {'gx','gy'}, use_global_device_ids=true, to_apply=%region_29.31 | all-reduce | flops 1 | bytes 8 | tf_op jit(solution)/shard_map/psum | solution.py:161
  1151.1 63.5 %psum.152 = f32[]{:T(128)} all-reduce(f32[]{:T(128)} %multiply_reduce_fusion.7), channel_id=1, replica_groups=mesh['gx'=16,'gy'=8] {'gx','gy'}, use_global_device_ids=true, to_apply=%region_31.33 | all-reduce | flops 1 | bytes 8 | tf_op jit(solution)/shard_map/psum | solution.py:164
  1223.1 4.9 collective-permute-start.30
  1241.2 66.1 %psum.153 = f32[]{:T(128)} all-reduce(f32[]{:T(128)} %get-tuple-element.246), channel_id=1, replica_groups=mesh['gx'=16,'gy'=8] {'gx','gy'}, use_global_device_ids=true, to_apply=%region_33.35 | all-reduce | flops 1 | bytes 8 | tf_op jit(solution)/shard_map/psum | solution.py:161
  1310.1 62.7 %psum.154 = f32[]{:T(128)} all-reduce(f32[]{:T(128)} %multiply_reduce_fusion.5), channel_id=1, replica_groups=mesh['gx'=16,'gy'=8] {'gx','gy'}, use_global_device_ids=true, to_apply=%region_35.37 | all-reduce | flops 1 | bytes 8 | tf_op jit(solution)/shard_map/psum | solution.py:161
  1376.4 64.1 %psum.155 = f32[]{:T(128)} all-reduce(f32[]{:T(128)} %get-tuple-element.244), channel_id=1, replica_groups=mesh['gx'=16,'gy'=8] {'gx','gy'}, use_global_device_ids=true, to_apply=%region_37.39 | all-reduce | flops 1 | bytes 8 | tf_op jit(solution)/shard_map/psum | solution.py:164
  1449.0 4.5 collective-permute-start.34
  1466.4 66.6 %psum.156 = f32[]{:T(128)} all-reduce(f32[]{:T(128)} %get-tuple-element.240), channel_id=1, replica_groups=mesh['gx'=16,'gy'=8] {'gx','gy'}, use_global_device_ids=true, to_apply=%region_39.41 | all-reduce | flops 1 | bytes 8 | tf_op jit(solution)/shard_map/psum | solution.py:161
  1534.5 63.9 %psum.157 = f32[]{:T(128)} all-reduce(f32[]{:T(128)} %multiply_reduce_fusion.2), channel_id=1, replica_groups=mesh['gx'=16,'gy'=8] {'gx','gy'}, use_global_device_ids=true, to_apply=%region_41.43 | all-reduce | flops 1 | bytes 8 | tf_op jit(solution)/shard_map/psum | solution.py:161
  1600.4 62.7 %psum.158 = f32[]{:T(128)} all-reduce(f32[]{:T(128)} %get-tuple-element.238), channel_id=1, replica_groups=mesh['gx'=16,'gy'=8] {'gx','gy'}, use_global_device_ids=true, to_apply=%region_43.45 | all-reduce | flops 1 | bytes 8 | tf_op jit(solution)/shard_map/psum | solution.py:161
  1666.4 64.1 %psum.159 = f32[]{:T(128)} all-reduce(f32[]{:T(128)} %multiply_reduce_fusion), channel_id=1, replica_groups=mesh['gx'=16,'gy'=8] {'gx','gy'}, use_global_device_ids=true, to_apply=%region_45.47 | all-reduce | flops 1 | bytes 8 | tf_op jit(solution)/shard_map/psum | solution.py:164
  (352 shorter events, 299.7 us)
Async XLA Ops:
  53.5 48.9 %all-to-all-start = ((f32[128,1,960]{2,1,0:T(1,128)}), f32[128,1,960]{2,1,0:T(1,128)}, u32[]{:S(2)}, u32[]{:S(2)}) async-start(f32[128,1,960]{2,1,0:T(1,128)} %reshape.820), calls=%async_computation | async-start | bytes 1048576 | tf_op jit(solution)/shard_map/all_to_all | solution.py:131
  73.2 10.6 collective-permute-start
  76.5 7.4 collective-permute-start.1
  77.9 12.4 collective-permute-start.4
  81.9 8.4 collective-permute-start.5
  84.1 12.2 collective-permute-start.2
  88.3 8.8 collective-permute-start.3
  90.4 7.9 collective-permute-start.6
  94.1 6.2 collective-permute-start.7
  132.7 24.8 %all-to-all-start.1 = ((f32[128,1,768]{2,1,0:T(1,128)}), f32[128,1,768]{2,1,0:T(1,128)}, u32[]{:S(2)}, u32[]{:S(2)}) async-start(f32[128,1,768]{2,1,0:T(1,128)} %reshape.822), calls=%async_computation.1 | async-start | bytes 786432 | tf_op jit(solution)/shard_map/all_to_all | solution.py:136
  284.1 4.5 collective-permute-start.9
  288.8 5.8 collective-permute-start.10
  292.4 6.2 collective-permute-start.11
  441.7 4.5 collective-permute-start.13
  446.4 6.5 collective-permute-start.14
  450.3 6.2 collective-permute-start.15
  661.6 4.6 collective-permute-start.16
  664.2 4.5 collective-permute-start.17
  670.1 10.1 collective-permute-start.18
  673.5 6.7 collective-permute-start.19
  972.5 4.5 collective-permute-start.21
  977.1 5.5 collective-permute-start.22
  980.6 6.2 collective-permute-start.23
  1061.6 4.5 collective-permute-start.25
  1066.3 6.8 collective-permute-start.26
  1070.8 6.2 collective-permute-start.27
  1218.5 4.5 collective-permute-start.29
  1223.1 6.8 collective-permute-start.30
  1228.0 6.2 collective-permute-start.31
  1443.5 4.7 collective-permute-start.33
  1449.0 10.7 collective-permute-start.34
  1453.5 6.5 collective-permute-start.35
  (63 other events, 1720.9 us)
where the time goes:
time: 1760 us; the launch traced here: 1750 us
  blocking collectives  1290 us (73%)
  other arithmetic  143 us (8%)
  local copies, waits for them, and re-layouts  122 us (7%)
  starting transfers between devices  115 us (7%)
  waiting for transfers between devices  54.2 us (3%)
  between operations  30.6 us (2%)
    psum x12, blocking collectives, shards(): product = lax.psum(jnp.sum(direction * earlier), ('gx', 'gy'))  777 us
    psum x6, blocking collectives, shards(): lax.psum(jnp.sum(direction * direction), ('gx', 'gy')) + norm_epsilon  380 us
    psum x2, blocking collectives, shards(): lax.psum(jnp.sum(residual_now * residual_now), ('gx', 'gy')) + norm_epsilon  129 us
    ppermute x18, starting transfers between devices, padded_2(): before = lax.ppermute(last, axis, up)  58.7 us
    ppermute x18, waiting for transfers between devices, padded_2(): after = lax.ppermute(initial, axis, down)  43.6 us
  transfers between devices with their start and end apart: 38, of which 16 were waited for; matrix products, arithmetic and copies ran while one was open for 1% of the time, Pallas kernels for 0%

commit v1 on v0

v1 whole, which is shorter than its diff:
```python
import functools

import jax
import jax.numpy as jnp
from jax import lax
from jax.experimental import pallas as pl
from jax.experimental.pallas import tpu as pltpu
from jax.sharding import PartitionSpec as P

NEWTON = 2
KRYLOV = 3
CAP = 64

STORAGE = 4.0
EPSILON = 1e-06

SHIFT = 3.0
SCALE = 3.0

MESH = pl.DeviceIdType.MESH
ROWS = 24
LANES = 640


def logistic(u):
    return 1.0 / (1.0 + jnp.exp(-u))


def ahead(x, axis):
    return pltpu.roll(x, x.shape[axis] - 1, axis)


def behind(x, axis):
    return pltpu.roll(x, 1, axis)


def krylov_weights(gram):
    def inner(vector, image):
        terms = [a * b for a, b in zip(vector, image) if a is not None]
        return functools.reduce(lambda a, b: a + b, terms)

    def image_of(vector):
        return [inner(vector, [gram[i][k] for i in range(4)]) for k in range(4)]

    beta = jnp.sqrt(gram[0][0] + EPSILON)
    basis = [[1.0 / beta, None, None, None]]
    images = [image_of(basis[0])]
    hessen = [[None] * KRYLOV for _ in range(KRYLOV + 1)]
    for j in range(KRYLOV):
        v = basis[j]
        w = [None] * 4
        for i in range(j + 2):
            if i <= j:
                w[i] = SHIFT * v[i]
            if i >= 1:
                term = SCALE * v[i - 1]
                w[i] = term if w[i] is None else w[i] + term
        for i in range(j + 1):
            product = inner(w, images[i])
            hessen[i][j] = product
            w = [a if b is None else a - product * b for a, b in zip(w, basis[i])]
        square = jnp.maximum(inner(w, image_of(w)), 0.0)
        length = jnp.sqrt(square + EPSILON)
        hessen[j + 1][j] = length
        if j + 1 < KRYLOV:
            basis.append([None if a is None else a / length for a in w])
            images.append(image_of(basis[-1]))

    def column(a, b):
        pairs = [(hessen[i][a], hessen[i][b]) for i in range(KRYLOV + 1)]
        terms = [x * y for x, y in pairs if x is not None and y is not None]
        return functools.reduce(lambda x, y: x + y, terms)

    factor = [[None] * KRYLOV for _ in range(KRYLOV)]
    for i in range(KRYLOV):
        for j in range(i + 1):
            value = column(i, j)
            for k in range(j):
                value = value - factor[i][k] * factor[j][k]
            factor[i][j] = jnp.sqrt(value) if i == j else value / factor[j][j]
    forward = []
    for row in range(KRYLOV):
        value = hessen[0][row] * beta
        for other in range(row):
            value = value - factor[row][other] * forward[other]
        forward.append(value / factor[row][row])
    y = [None] * KRYLOV
    for row in reversed(range(KRYLOV)):
        value = forward[row]
        for other in range(row + 1, KRYLOV):
            value = value - factor[other][row] * y[other]
        y[row] = value / factor[row][row]
    weights = []
    for i in range(KRYLOV):
        terms = [y[j] * basis[j][i] for j in range(KRYLOV) if basis[j][i] is not None]
        weights.append(functools.reduce(lambda a, b: a + b, terms))
    return weights


def kernel(
    sizes,
    head_ref,
    soil_ref,
    table_ref,
    forcing_ref,
    canopy_ref,
    slot_ref,
    out_ref,
    flux_ref,
    send_c,
    recv_c,
    split,
    records,
    head,
    soil,
    conduct,
    slope,
    ksat,
    steep,
    cap,
    coef,
    basis,
    wet,
    theta_old,
    source,
    mask,
    send_x,
    recv_x,
    send_y,
    recv_y,
    part,
    gather_x,
    gather_y,
    sem_c,
    sem_x,
    sem_y,
    sem_gx,
    sem_gy,
):
    size_x, size_y = sizes
    devices = size_x * size_y
    layers = head_ref.shape[0]
    half = layers // 2
    gx, gy = lax.axis_index("gx"), lax.axis_index("gy")
    me = gx * size_y + gy

    def device(d):
        return (d // size_y, lax.rem(d, size_y))

    barrier = pltpu.get_barrier_semaphore()

    def greet(i, carry):
        pl.semaphore_signal(
            barrier, inc=1, device_id=device(lax.rem(me + i, devices)), device_id_type=MESH
        )
        return carry

    lax.fori_loop(1, devices, greet, 0)

    lane8 = lax.broadcasted_iota(jnp.int32, (8, 128), 1)
    low8 = lane8 < CAP

    def pack(q, carry):
        lanes = pl.ds(pl.multiple_of(q * 128, 128), 128)
        first, second = canopy_ref[0:8, lanes], canopy_ref[5:13, lanes]
        send_c[2 * q] = jnp.where(low8, first, pltpu.roll(second, CAP, 1))
        send_c[2 * q + 1] = jnp.where(low8, pltpu.roll(first, CAP, 1), second)
        return carry

    lax.fori_loop(0, devices // 2, pack, 0)
    recv_c[pl.ds(pl.multiple_of(me * 8, 8), 8), :] = send_c[me]

    row = lax.broadcasted_iota(jnp.int32, (ROWS, LANES), 0)
    col = lax.broadcasted_iota(jnp.int32, (ROWS, LANES), 1)
    one, zero = jnp.float32(1.0), jnp.float32(0.0)
    has_next_x = jnp.where(gx < size_x - 1, one, zero)
    has_prev_x = jnp.where(gx > 0, one, zero)
    has_next_y = jnp.where(gy < size_y - 1, one, zero)
    has_prev_y = jnp.where(gy > 0, one, zero)
    inside_x = jnp.where(row < 16, 1.0, jnp.where(row < 20, has_next_x, has_prev_x))
    inside_y = jnp.where(
        col < 512,
        1.0,
        jnp.where(col < 516, has_next_y, jnp.where(col >= LANES - 4, has_prev_y, 0.0)),
    )
    mask[...] = inside_x * inside_y

    def own(ref, k):
        return ref[k, 0:16, 0:512]

    def clear(k, carry):
        head[k] = jnp.zeros((ROWS, LANES), jnp.float32)
        soil[k] = jnp.zeros((ROWS, LANES), jnp.float32)
        basis[0, k] = jnp.zeros((ROWS, LANES), jnp.float32)
        head[k, 0:16, 0:512] = head_ref[k]
        soil[k, 0:16, 0:512] = soil_ref[k].astype(jnp.float32)
        return carry

    lax.fori_loop(0, layers, clear, 0)

    sub512 = lax.broadcasted_iota(jnp.int32, (8, 512), 0)
    early = sub512 < 4

    def wrap(value, size):
        return lax.rem(value + size, size)

    next_x, prev_x = (wrap(gx + 1, size_x), gy), (wrap(gx - 1, size_x), gy)
    next_y, prev_y = (gx, wrap(gy + 1, size_y)), (gx, wrap(gy - 1, size_y))

    def copies(send, recv, sem, number, slot, count, targets):
        return [
            pltpu.make_async_remote_copy(
                src_ref=send.at[side, pl.ds(slot, count)],
                dst_ref=recv.at[side, pl.ds(slot, count)],
                send_sem=sem.at[0, number, side],
                recv_sem=sem.at[1, number, side],
                device_id=target,
                device_id_type=MESH,
            )
            for side, target in enumerate(targets)
        ]

    def start_x(number, slot, fields):
        def pack_rows(k, carry):
            for f, (ref, index) in enumerate(fields):
                at = lambda k: ref[index + (k, slice(0, 16), slice(0, 512))]
                upper, lower = at(k), at(k + half)
                send_x[0, slot + f, k] = jnp.where(early, pltpu.roll(lower[8:16], 4, 0), upper[8:16])
                send_x[1, slot + f, k] = jnp.where(early, upper[0:8], pltpu.roll(lower[0:8], 4, 0))
            return carry

        lax.fori_loop(0, half, pack_rows, 0)
        moves = copies(send_x, recv_x, sem_x, number, slot, len(fields), (next_x, prev_x))
        for move in moves:
            move.start()
        return moves

    def finish_x(moves, slot, fields):
        for move in moves:
            move.wait()
        edge = mask[16:24, 0:512]

        def place_rows(k, carry):
            for f, (ref, index) in enumerate(fields):
                before, after = recv_x[0, slot + f, k], recv_x[1, slot + f, k]
                ref[index + (k, slice(16, 24), slice(0, 512))] = edge * jnp.where(early, after, before)
                other = pltpu.roll(jnp.where(early, before, after), 4, 0)
                ref[index + (k + half, slice(16, 24), slice(0, 512))] = edge * other
            return carry

        lax.fori_loop(0, half, place_rows, 0)

    lane24 = lax.broadcasted_iota(jnp.int32, (ROWS, 128), 1)
    group24 = lane24 // 4

    def start_y(number, slot, fields):
        for f, (ref, index) in enumerate(fields):
            up = jnp.zeros((ROWS, 128), jnp.float32)
            down = jnp.zeros((ROWS, 128), jnp.float32)
            for k in range(layers):
                last = ref[index + (k, slice(0, ROWS), slice(384, 512))]
                first = ref[index + (k, slice(0, ROWS), slice(0, 128))]
                here = group24 == k
                up = jnp.where(here, pltpu.roll(last, 4 * k + 4, 1), up)
                down = jnp.where(here, pltpu.roll(first, 4 * k, 1) if k else first, down)
            send_y[0, slot + f] = up
            send_y[1, slot + f] = down
        moves = copies(send_y, recv_y, sem_y, number, slot, len(fields), (next_y, prev_y))
        for move in moves:
            move.start()
        return moves

    def finish_y(moves, slot, fields):
        for move in moves:
            move.wait()
        edge = mask[:, 512:640]
        for f, (ref, index) in enumerate(fields):
            before, after = recv_y[0, slot + f], recv_y[1, slot + f]
            for k in range(layers):
                left = pltpu.roll(before, 128 - (4 * k + 4), 1)
                right = pltpu.roll(after, 128 - 4 * k, 1) if k else after
                both = jnp.where(lane24 < 4, right, jnp.where(lane24 >= 124, left, 0.0))
                ref[index + (k, slice(0, ROWS), slice(512, 640))] = edge * both

    def exchange(number, slot, fields):
        finish_x(start_x(number, slot, fields), slot, fields)
        finish_y(start_y(number, slot, fields), slot, fields)

    pl.semaphore_wait(barrier, devices - 1)

    opening = [(head, ()), (soil, ())]
    moves = start_x(0, 0, opening)

    def scatter(i, carry):
        d = lax.rem(me + i, devices)
        pltpu.make_async_remote_copy(
            src_ref=send_c.at[d],
            dst_ref=recv_c.at[pl.ds(pl.multiple_of(me * 8, 8), 8)],
            send_sem=sem_c.at[0],
            recv_sem=sem_c.at[1],
            device_id=device(d),
            device_id_type=MESH,
        ).start()
        return carry

    lax.fori_loop(1, devices, scatter, 0)

    finish_x(moves, 0, opening)
    finish_y(start_y(0, 0, opening), 0, opening)

    def look_up(k, carry):
        kind = soil[k]
        values = [jnp.zeros((ROWS, LANES), jnp.float32) for _ in range(3)]
        for c in range(table_ref.shape[1]):
            match = kind == float(c)
            values = [jnp.where(match, table_ref[p, c], v) for p, v in enumerate(values)]
        ksat[k] = values[0] * mask[...]
        steep[k] = values[1]
        cap[k] = values[2]
        return carry

    lax.fori_loop(0, layers, look_up, 0)

    def saturate(first):
        def layer(k, carry):
            a, ks, c = steep[k], ksat[k], cap[k]
            s = logistic(a * head[k])
            rise = a * s * (1.0 - s)
            conduct[k] = ks * (0.1 + 0.9 * s * s)
            slope[k] = 0.9 * ks * s * rise
            coef[0, k] = STORAGE * c * rise
            theta = (c * s)[0:16, 0:512]
            if first:
                wet[k] = s[0:16, 0:512]
                theta_old[k] = theta
            else:
                basis[0, k, 0:16, 0:512] = STORAGE * (theta - theta_old[k]) - source[k]
            return carry

        lax.fori_loop(0, layers, layer, 0)

    def linearize(first):
        scaled = mask[...] * (1.0 / SCALE)

        def layer(k, carry):
            h, kk, dk = head[k], conduct[k], slope[k]
            diagonal = coef[0, k] - SHIFT
            total = None
            for axis, at in ((0, 1), (1, 3)):
                drop = h - ahead(h, axis)
                mean = 0.5 * (kk + ahead(kk, axis))
                mine = dk * drop + mean
                other = ahead(dk, axis) * drop - mean
                flow = mean * drop
                net = flow - behind(flow, axis)
                total = net if total is None else total + net
                diagonal = diagonal + mine - behind(other, axis)
                coef[at, k] = other * scaled
                coef[at + 1, k] = -behind(mine, axis) * scaled
            below, above = jnp.minimum(k + 1, layers - 1), jnp.maximum(k - 1, 0)
            bottom, top = k == layers - 1, k == 0
            drop = h - head[below] + 1.0
            mean = 0.5 * (kk + conduct[below])
            mine = jnp.where(bottom, 2.0 * dk, dk * drop + mean)
            other = jnp.where(bottom, 0.0, slope[below] * drop - mean)
            flow = jnp.where(bottom, kk, mean * drop)
            diagonal = diagonal + mine
            coef[5, k] = other * scaled
            total = total + flow
            drop = head[above] - h + 1.0
            mean = 0.5 * (kk + conduct[above])
            mine = jnp.where(top, 0.0, slope[above] * drop + mean)
            other = jnp.where(top, 0.0, dk * drop - mean)
            flow = jnp.where(top, 0.0, mean * drop)
            diagonal = diagonal - other
            coef[6, k] = -mine * scaled
            total = total - flow
            coef[0, k] = diagonal * scaled
            if first:
                basis[0, k, 0:16, 0:512] = total[0:16, 0:512]
            else:
                basis[0, k, 0:16, 0:512] += total[0:16, 0:512]
            return carry

        lax.fori_loop(0, layers, layer, 0)

    saturate(True)
    linearize(True)

    everything = pltpu.make_async_copy(
        recv_c.at[pl.ds(0, 8 * (devices - 1))], recv_c.at[pl.ds(0, 8 * (devices - 1))], sem_c.at[1]
    )
    everything.wait()
    blocks = devices // 4
    low = lax.broadcasted_iota(jnp.int32, (blocks, 128), 1) < CAP

    def put(r, left, right):
        value = jnp.concatenate([left, right], axis=1)
        high = value.astype(jnp.bfloat16)
        split[blocks * r : blocks * (r + 1), 0:256] = high
        split[blocks * r : blocks * (r + 1), 256:512] = (value - high.astype(jnp.float32)).astype(
            jnp.bfloat16
        )

    for r in range(8):
        plain = [recv_c[pl.ds(8 * c + r, blocks, stride=32), :] for c in range(4)]
        moved = [pltpu.roll(x, CAP, 1) for x in plain]
        put(r, jnp.where(low, plain[0], moved[1]), jnp.where(low, plain[2], moved[3]))
        if r >= 3:
            put(r + 5, jnp.where(low, moved[0], plain[1]), jnp.where(low, moved[2], plain[3]))

    within = lax.broadcasted_iota(jnp.int32, (256, 512), 0)
    which = lax.broadcasted_iota(jnp.int32, (blocks, 512), 0)

    def select(x, carry):
        slot = jnp.maximum(slot_ref[pl.ds(x, 1), :], 0)
        hot = jnp.where(within == (slot & 255), 1.0, 0.0).astype(jnp.bfloat16)
        found = jnp.dot(
            split[...], jnp.concatenate([hot, hot], axis=0), preferred_element_type=jnp.float32
        )
        match = which == (slot >> 8)
        for r in range(13):
            piece = jnp.where(match, found[blocks * r : blocks * (r + 1)], 0.0)
            records[r, pl.ds(x, 1), :] = jnp.sum(piece, axis=0, keepdims=True)
        return carry

    lax.fori_loop(0, 16, select, 0)

    sunlight, air, humidity, rainfall = (forcing_ref[i] for i in range(4))
    leaf, albedo, resist = (records[i] for i in range(3))
    total, roots = jnp.zeros_like(leaf), jnp.zeros_like(leaf)
    for k in range(layers):
        total = total + records[3 + k] * wet[k]
        roots = roots + records[3 + k]
    conductance = total / roots * leaf / (leaf + resist)
    exchange_coef = 0.5 + 0.3 * leaf
    radiation = (1.0 - albedo) * sunlight + 0.3
    surface = air
    for _ in range(2):
        vapour = 0.5 * jnp.exp(2.0 * (surface - air))
        square = surface * surface
        excess = (
            radiation
            - 0.3 * square * square
            - exchange_coef * (surface - air)
            - conductance * (vapour - humidity)
        )
        tangent = -1.2 * square * surface - exchange_coef - 2.0 * conductance * vapour
        surface = surface - excess / tangent
    evaporation = conductance * (0.5 * jnp.exp(2.0 * (surface - air)) - humidity)
    ks_top = own(ksat, 0)
    infiltration = rainfall * ks_top / (rainfall + ks_top)
    land = slot_ref[...] >= 0
    evaporation = jnp.where(land, evaporation, 0.0)
    infiltration = jnp.where(land, infiltration, 0.0)
    flux_ref[0] = evaporation
    flux_ref[1] = infiltration
    share = evaporation / total
    for k in range(layers):
        gain = -jnp.where(land, share * records[3 + k] * wet[k], 0.0)
        if k == 0:
            gain = gain + infiltration
        source[k] = gain
        basis[0, k, 0:16, 0:512] -= gain

    def fold(product):
        tall = product[0:8] + product[8:16]
        return (tall[:, 0:128] + tall[:, 128:256]) + (tall[:, 256:384] + tall[:, 384:512])

    def accumulate(n, at, sums):
        for i, value in enumerate(sums):
            part[n, 0, at + i : at + i + 1, :] = jnp.sum(value, axis=0, keepdims=True)

    def matvec(n, j, at):
        def layer(k, carry):
            v = basis[j, k]
            below, above = jnp.minimum(k + 1, layers - 1), jnp.maximum(k - 1, 0)
            w = coef[0, k] * v
            w = w + coef[1, k] * ahead(v, 0) + coef[2, k] * behind(v, 0)
            w = w + coef[3, k] * ahead(v, 1) + coef[4, k] * behind(v, 1)
            w = w + coef[5, k] * basis[j, below] + coef[6, k] * basis[j, above]
            if j + 1 < KRYLOV:
                basis[j + 1, k] = w
            mine = w[0:16, 0:512]
            sums = [fold(mine * basis[i, k, 0:16, 0:512]) for i in range(j + 1)]
            sums.append(fold(mine * mine))
            return tuple(a + b for a, b in zip(carry, sums))

        zeros = tuple(jnp.zeros((8, 128), jnp.float32) for _ in range(j + 2))
        accumulate(n, at, lax.fori_loop(0, layers, layer, zeros))

    def square_of_start(n):
        def layer(k, carry):
            value = own(basis.at[0], k)
            return carry + fold(value * value)

        accumulate(n, 0, [lax.fori_loop(0, layers, layer, jnp.zeros((8, 128), jnp.float32))])

    def reduce_all(n):
        def along(stage, gather, sem, here, size, target):
            mine = part.at[n, stage]
            gather[n, here] = mine[...]

            def send(i, carry):
                pltpu.make_async_remote_copy(
                    src_ref=mine,
                    dst_ref=gather.at[n, here],
                    send_sem=sem.at[0, n],
                    recv_sem=sem.at[1, n],
                    device_id=target(lax.rem(here + i, size)),
                    device_id_type=MESH,
                ).start()
                return carry

            lax.fori_loop(1, size, send, 0)
            rest = gather.at[n, pl.ds(0, size - 1)]
            pltpu.make_async_copy(rest, rest, sem.at[1, n]).wait()
            total = gather[n, 0]
            for i in range(1, size):
                total = total + gather[n, i]
            return total

        part[n, 1] = along(0, gather_x, sem_gx, gx, size_x, lambda d: (d, gy))
        total = along(1, gather_y, sem_gy, gy, size_y, lambda d: (gx, d))
        return jnp.sum(total, axis=1, keepdims=True)

    for n in range(NEWTON):
        if n:
            saturate(False)
            linearize(False)
        field = [(basis, (0,))]
        moves = start_x(1 + n, 2 + n, field)
        part[n, 0] = jnp.zeros((16, 128), jnp.float32)
        square_of_start(n)
        finish_x(moves, 2 + n, field)
        finish_y(start_y(1 + n, 2 + n, field), 2 + n, field)
        for j, at in ((0, 1), (1, 3), (2, 6)):
            matvec(n, j, at)
        sums = reduce_all(n)
        gram = [[None] * 4 for _ in range(4)]
        at = 0
        for i in range(4):
            for j in range(i + 1):
                gram[i][j] = gram[j][i] = sums[at : at + 1, :]
                at += 1
        weights = krylov_weights(gram)

        def update(k, carry):
            step = [weights[i] * own(basis.at[i], k) for i in range(KRYLOV)]
            value = own(head, k)
            for term in step:
                value = value - term
            if n + 1 < NEWTON:
                head[k, 0:16, 0:512] = value
            else:
                out_ref[k] = value
            return carry

        lax.fori_loop(0, layers, update, 0)
        if n + 1 < NEWTON:
            exchange(3 + n, 4 + n, [(head, ())])

    sent = send_c.at[pl.ds(0, devices - 1)]
    pltpu.make_async_copy(sent, sent, sem_c.at[0]).wait()
    for n in range(NEWTON):
        sent = gather_x.at[n, pl.ds(0, size_x - 1)]
        pltpu.make_async_copy(sent, sent, sem_gx.at[0, n]).wait()
        sent = gather_y.at[n, pl.ds(0, size_y - 1)]
        pltpu.make_async_copy(sent, sent, sem_gy.at[0, n]).wait()


def shards(sizes, head_old, soil_type, soil_table, forcing, canopy, column_slot):
    layers = head_old.shape[0]
    devices = sizes[0] * sizes[1]
    f32 = jnp.float32
    wide = (layers, ROWS, LANES)
    tile = (layers, 16, 512)
    vmem = pl.BlockSpec(memory_space=pltpu.VMEM)
    return pl.pallas_call(
        functools.partial(kernel, sizes),
        out_shape=(
            jax.ShapeDtypeStruct(head_old.shape, f32),
            jax.ShapeDtypeStruct((2, 16, 512), f32),
        ),
        in_specs=[vmem, vmem, pl.BlockSpec(memory_space=pltpu.SMEM), vmem, vmem, vmem],
        out_specs=(vmem, vmem),
        scratch_shapes=[
            pltpu.VMEM((devices, 8, 128), f32),
            pltpu.VMEM((devices * 8, 128), f32),
            pltpu.VMEM((13 * (devices // 4), 512), jnp.bfloat16),
            pltpu.VMEM((13, 16, 512), f32),
            pltpu.VMEM(wide, f32),
            pltpu.VMEM(wide, f32),
            pltpu.VMEM(wide, f32),
            pltpu.VMEM(wide, f32),
            pltpu.VMEM(wide, f32),
            pltpu.VMEM(wide, f32),
            pltpu.VMEM(wide, f32),
            pltpu.VMEM((7,) + wide, f32),
            pltpu.VMEM((KRYLOV,) + wide, f32),
            pltpu.VMEM(tile, f32),
            pltpu.VMEM(tile, f32),
            pltpu.VMEM(tile, f32),
            pltpu.VMEM((ROWS, LANES), f32),
            pltpu.VMEM((2, 5, layers // 2, 8, 512), f32),
            pltpu.VMEM((2, 5, layers // 2, 8, 512), f32),
            pltpu.VMEM((2, 5, ROWS, 128), f32),
            pltpu.VMEM((2, 5, ROWS, 128), f32),
            pltpu.VMEM((NEWTON, 2, 16, 128), f32),
            pltpu.VMEM((NEWTON, sizes[0], 16, 128), f32),
            pltpu.VMEM((NEWTON, sizes[1], 16, 128), f32),
            pltpu.SemaphoreType.DMA((2,)),
            pltpu.SemaphoreType.DMA((2, 4, 2)),
            pltpu.SemaphoreType.DMA((2, 4, 2)),
            pltpu.SemaphoreType.DMA((2, NEWTON)),
            pltpu.SemaphoreType.DMA((2, NEWTON)),
        ],
        compiler_params=pltpu.CompilerParams(collective_id=0, has_side_effects=True),
        name="coupled_step",
    )(head_old, soil_type, soil_table, forcing, canopy, column_slot)


def solution(mesh):
    sizes = (mesh.shape["gx"], mesh.shape["gy"])
    return jax.shard_map(
        functools.partial(shards, sizes),
        mesh=mesh,
        in_specs=(
            P(None, "gx", "gy"),
            P(None, "gx", "gy"),
            P(),
            P(None, "gx", "gy"),
            P(None, ("gx", "gy")),
            P("gx", "gy"),
        ),
        out_specs=(P(None, "gx", "gy"), P(None, "gx", "gy")),
        check_vma=False,
    )
```

time: 1760 us -> 94.5 us (0.05)
  blocking collectives: 1290 us -> 0 us
  other arithmetic: 143 us -> 0 us
  local copies, waits for them, and re-layouts: 122 us -> 2.38 us
  starting transfers between devices: 115 us -> 0 us
  Pallas kernels: 0 us -> 91.4 us
  waiting for transfers between devices: 54.2 us -> 0 us
  between operations: 30.6 us -> 0.65 us
    psum x20 -> x0, blocking collectives: 1290 us -> none  [the longest x12 777 us: shards(): product = lax.psum(jnp.sum(direction * earlier), ('gx', 'gy'))]
    pallas_call x0 -> x1, Pallas kernels: none -> 91.4 us  [shards(): pl.pallas_call(functools.partial(kernel, sizes), out_shape=(jax.ShapeDtyp...]
    ppermute x36 -> x0, starting transfers between devices: 89.6 us -> none  [the longest x18 58.7 us: padded_2(): before = lax.ppermute(last, axis, up)]
    reduce_sum x21 -> x0, other arithmetic: 58.4 us -> none  [the longest x12 34.1 us: shards(): product = lax.psum(jnp.sum(direction * earlier), ('gx', 'gy'))]
    ppermute x36 -> x0, waiting for transfers between devices: 43.6 us -> none  [the longest x18 43.6 us: padded_2(): after = lax.ppermute(initial, axis, down)]
    scatter x19 -> x0, local copies, waits for them, and re-layouts: 36.6 us -> none  [the longest x1 23 us: shards(): buffer = jnp.zeros((outgoing.shape[0], canopy.shape[1]), jnp.float32).at[...]
    gather x1 -> x0, local copies, waits for them, and re-layouts: 29.9 us -> none  [shards(): jnp.take(returned, flat_slot, axis=1).reshape(layers + 2, rows_x, rows_y)]
    all_to_all x2 -> x0, starting transfers between devices: 24.9 us -> none  [the longest x1 13 us: shards(): lax.all_to_all(results, ('gx', 'gy'), split_axis=1, concat_axis=1, tiled=...]
  transfers between devices with their start and end apart: 38 -> 0, of which waited for: 16 -> 0; matrix products, arithmetic and copies ran while one was open for 1% -> 0% of each run, Pallas kernels for 0% -> 0%
where the time goes in v1:
time: 94.5 us; the launch traced here: 94.4 us
  Pallas kernels  91.4 us (97%)
  local copies, waits for them, and re-layouts  2.38 us (3%)
    pallas_call x1, Pallas kernels, shards(): pl.pallas_call(functools.partial(kernel, sizes), out_shape=(jax.ShapeDtyp...  91.4 us
    unnamed x4, local copies, waits for them, and re-layouts  2.38 us

profile of v1, /device:TPU:1, one launch (start us, length us, event | category | flops | bytes accessed | tf_op | source)
XLA Modules:
  0.0 94.4 jit_solution(1099660112882612645)
XLA Ops:
  0.6 91.4 %coupled_step.1 = (f32[10,16,512]{2,1,0:T(8,128)}, f32[2,16,512]{2,1,0:T(8,128)}) custom-call(f32[10,16,512]{2,1,0:T(8,128)} %head_ref.1, s32[10,16,512]{2,1,0:T(8,128)} %soil_ref.1, f32[3,12]{1,0:T(4,128)} %table_ref.1, f32[4,16,512]{2,1,0:T(8,128)} %forcing_ref.1, f32[13,8192]{1,0:T(8,128)} %canopy_ref.1, s32[16,512]{1,0:T(8,128)} %slot_ref.1), custom_call_target="tpu_custom_call" | custom-call | tf_op jit(solution)/shard_map/coupled_step/pallas_call | solution.py:579
  92.0 0.0 copy-start
  92.0 1.7 %copy.10 = f32[10,16,512]{2,1,0:T(8,128)} copy(f32[10,16,512]{2,1,0:T(8,128)} %get-tuple-element.4) | data formatting | bytes 655360
  93.8 0.0 copy-done
  93.8 0.6 copy.11
Async XLA Ops:
  92.0 1.8 %copy-start = (f32[2,16,512]{2,1,0:T(8,128)S(1)}, f32[2,16,512]{2,1,0:T(8,128)}, u32[]{:S(2)}) copy-start(f32[2,16,512]{2,1,0:T(8,128)} %get-tuple-element.5) | copy-start | bytes 196612

commit v2 on v1

v2 whole, which is shorter than its diff:
```python
import functools

import jax
import jax.numpy as jnp
from jax import lax
from jax.experimental import pallas as pl
from jax.experimental.pallas import tpu as pltpu
from jax.sharding import PartitionSpec as P

NEWTON = 2
KRYLOV = 3
CAP = 64

STORAGE = 4.0
EPSILON = 1e-06

SHIFT = 3.0
SCALE = 3.0

MESH = pl.DeviceIdType.MESH
HALO = 3
ROWS = 24
LANES = 640


def logistic(u):
    return 1.0 / (1.0 + jnp.exp(-u))


def ahead(x, axis):
    return pltpu.roll(x, x.shape[axis] - 1, axis)


def behind(x, axis):
    return pltpu.roll(x, 1, axis)


def krylov_weights(gram):
    def inner(vector, image):
        terms = [a * b for a, b in zip(vector, image) if a is not None]
        return functools.reduce(lambda a, b: a + b, terms)

    def image_of(vector):
        return [inner(vector, [gram[i][k] for i in range(4)]) for k in range(4)]

    beta = jnp.sqrt(gram[0][0] + EPSILON)
    basis = [[1.0 / beta, None, None, None]]
    images = [image_of(basis[0])]
    hessen = [[None] * KRYLOV for _ in range(KRYLOV + 1)]
    for j in range(KRYLOV):
        v = basis[j]
        w = [None] * 4
        for i in range(j + 2):
            if i <= j:
                w[i] = SHIFT * v[i]
            if i >= 1:
                term = SCALE * v[i - 1]
                w[i] = term if w[i] is None else w[i] + term
        for i in range(j + 1):
            product = inner(w, images[i])
            hessen[i][j] = product
            w = [a if b is None else a - product * b for a, b in zip(w, basis[i])]
        square = jnp.maximum(inner(w, image_of(w)), 0.0)
        length = jnp.sqrt(square + EPSILON)
        hessen[j + 1][j] = length
        if j + 1 < KRYLOV:
            basis.append([None if a is None else a / length for a in w])
            images.append(image_of(basis[-1]))

    def column(a, b):
        pairs = [(hessen[i][a], hessen[i][b]) for i in range(KRYLOV + 1)]
        terms = [x * y for x, y in pairs if x is not None and y is not None]
        return functools.reduce(lambda x, y: x + y, terms)

    factor = [[None] * KRYLOV for _ in range(KRYLOV)]
    for i in range(KRYLOV):
        for j in range(i + 1):
            value = column(i, j)
            for k in range(j):
                value = value - factor[i][k] * factor[j][k]
            factor[i][j] = jnp.sqrt(value) if i == j else value / factor[j][j]
    forward = []
    for row in range(KRYLOV):
        value = hessen[0][row] * beta
        for other in range(row):
            value = value - factor[row][other] * forward[other]
        forward.append(value / factor[row][row])
    y = [None] * KRYLOV
    for row in reversed(range(KRYLOV)):
        value = forward[row]
        for other in range(row + 1, KRYLOV):
            value = value - factor[other][row] * y[other]
        y[row] = value / factor[row][row]
    weights = []
    for i in range(KRYLOV):
        terms = [y[j] * basis[j][i] for j in range(KRYLOV) if basis[j][i] is not None]
        weights.append(functools.reduce(lambda a, b: a + b, terms))
    return weights


def kernel(
    sizes,
    head_in,
    soil_in,
    table_ref,
    forcing_in,
    canopy_in,
    slot_in,
    out_ref,
    flux_ref,
    soil_ref,
    forcing_ref,
    canopy_ref,
    slot_ref,
    send_c,
    recv_c,
    split,
    hot,
    records,
    head,
    soil,
    conduct,
    slope,
    ksat,
    steep,
    cap,
    coef,
    basis,
    wet,
    theta_old,
    source,
    mask,
    send_x,
    recv_x,
    send_y,
    recv_y,
    recv_k,
    part,
    gather_x,
    gather_y,
    sem_in,
    sem_c,
    sem_e,
    sem_gx,
    sem_gy,
):
    size_x, size_y = sizes
    devices = size_x * size_y
    layers = out_ref.shape[0]
    gx, gy = lax.axis_index("gx"), lax.axis_index("gy")
    me = gx * size_y + gy

    loads = [
        pltpu.make_async_copy(src, dst, sem_in.at[i])
        for i, (src, dst) in enumerate(
            (
                (canopy_in, canopy_ref),
                (head_in, head.at[:, 0:16, 0:512]),
                (soil_in, soil_ref),
                (slot_in, slot_ref),
                (forcing_in, forcing_ref),
            )
        )
    ]
    for load in loads:
        load.start()

    def wrap(value, size):
        return lax.rem(value + size, size)

    def others(visit):
        for dy in range(1, size_y):
            visit(gx, lax.rem(gy + dy, size_y))

        def ring(i, carry):
            far = (i + 1) // 2
            x = wrap(gx + jnp.where(lax.rem(i, 2) == 1, far, -far), size_x)
            for dy in range(size_y):
                visit(x, lax.rem(gy + dy, size_y))
            return carry

        lax.fori_loop(1, size_x, ring, 0)

    barrier = pltpu.get_barrier_semaphore()
    others(lambda x, y: pl.semaphore_signal(barrier, inc=1, device_id=(x, y), device_id_type=MESH))

    row = lax.broadcasted_iota(jnp.int32, (ROWS, LANES), 0)
    col = lax.broadcasted_iota(jnp.int32, (ROWS, LANES), 1)
    one, zero = jnp.float32(1.0), jnp.float32(0.0)
    has_next_x = jnp.where(gx < size_x - 1, one, zero)
    has_prev_x = jnp.where(gx > 0, one, zero)
    has_next_y = jnp.where(gy < size_y - 1, one, zero)
    has_prev_y = jnp.where(gy > 0, one, zero)
    inside_x = jnp.where(
        row < 16,
        1.0,
        jnp.where(row < 16 + HALO, has_next_x, jnp.where(row >= ROWS - HALO, has_prev_x, 0.0)),
    )
    inside_y = jnp.where(
        col < 512,
        1.0,
        jnp.where(col < 512 + HALO, has_next_y, jnp.where(col >= LANES - HALO, has_prev_y, 0.0)),
    )
    mask[...] = inside_x * inside_y

    def own(ref, k):
        return ref[k, 0:16, 0:512]

    def clear(k, carry):
        for ref in (head, soil, basis.at[0]):
            ref[k, 16:24, 0:512] = jnp.zeros((8, 512), jnp.float32)
            ref[k, 0:24, 512:640] = jnp.zeros((24, 128), jnp.float32)
        return carry

    lax.fori_loop(0, layers, clear, 0)
    for side in range(2):
        for slot in range(5):
            send_x[side, slot, 24:32, :] = jnp.zeros((8, 512), jnp.float32)

    lane8 = lax.broadcasted_iota(jnp.int32, (8, 128), 1)
    low8 = lane8 < CAP

    def pack(q, carry):
        lanes = pl.ds(pl.multiple_of(q * 128, 128), 128)
        first, second = canopy_ref[0:8, lanes], canopy_ref[5:13, lanes]
        send_c[2 * q] = jnp.where(low8, first, pltpu.roll(second, CAP, 1))
        send_c[2 * q + 1] = jnp.where(low8, pltpu.roll(first, CAP, 1), second)
        return carry

    loads[0].wait()
    lax.fori_loop(0, devices // 2, pack, 0, unroll=4)
    recv_c[pl.ds(pl.multiple_of(me * 8, 8), 8), :] = send_c[me]

    next_x, prev_x = wrap(gx + 1, size_x), wrap(gx - 1, size_x)
    next_y, prev_y = wrap(gy + 1, size_y), wrap(gy - 1, size_y)
    lane16 = lax.broadcasted_iota(jnp.int32, (16, 128), 1)
    group16 = lane16 // 4
    lane24 = lax.broadcasted_iota(jnp.int32, (ROWS, 128), 1)
    early8 = lax.broadcasted_iota(jnp.int32, (8, 128), 0) < 4

    def start(number, slot, fields):
        for f, (ref, index) in enumerate(fields):
            up = jnp.zeros((16, 128), jnp.float32)
            down = jnp.zeros((16, 128), jnp.float32)
            for k in range(layers):
                rows = slice(HALO * k, HALO * (k + 1))
                send_x[0, slot + f, rows, :] = ref[index + (k, slice(16 - HALO, 16), slice(0, 512))]
                send_x[1, slot + f, rows, :] = ref[index + (k, slice(0, HALO), slice(0, 512))]
                last = ref[index + (k, slice(0, 16), slice(384, 512))]
                first = ref[index + (k, slice(0, 16), slice(0, 128))]
                here = group16 == k
                up = jnp.where(here, pltpu.roll(last, 4 * k + 4, 1), up)
                down = jnp.where(here, pltpu.roll(first, 4 * k, 1) if k else first, down)
            send_y[0, slot + f] = up
            send_y[1, slot + f] = down
        slots = pl.ds(slot, len(fields))
        plan = []
        for side, y in enumerate((next_y, prev_y)):
            for turn, x in enumerate((next_x, prev_x)):
                edge = pl.ds(8 * (1 - turn), 8)
                plan.append(
                    (send_y.at[side, slots, edge], recv_k.at[side, turn, slots], (x, y))
                )
        for side, x in enumerate((next_x, prev_x)):
            plan.append((send_x.at[side, slots], recv_x.at[side, slots], (x, gy)))
        for side, y in enumerate((next_y, prev_y)):
            plan.append((send_y.at[side, slots], recv_y.at[side, slots], (gx, y)))
        moves = [
            pltpu.make_async_remote_copy(
                src_ref=src,
                dst_ref=dst,
                send_sem=sem_e.at[0, number, i],
                recv_sem=sem_e.at[1, number, i],
                device_id=target,
                device_id_type=MESH,
            )
            for i, (src, dst, target) in enumerate(plan)
        ]
        for move in moves:
            move.start()
        return moves

    def finish(moves, slot, fields):
        for move in moves[6:] + moves[:4]:
            move.wait()
        edge = mask[:, 512:640]
        for f, (ref, index) in enumerate(fields):
            sides = [
                jnp.concatenate(
                    [
                        recv_y[side, slot + f],
                        jnp.where(early8, recv_k[side, 1, slot + f], recv_k[side, 0, slot + f]),
                    ],
                    axis=0,
                )
                for side in range(2)
            ]
            for k in range(layers):
                left = pltpu.roll(sides[0], 128 - (4 * k + 4), 1)
                right = pltpu.roll(sides[1], 128 - 4 * k, 1) if k else sides[1]
                both = jnp.where(lane24 < 64, right, left)
                ref[index + (k, slice(0, ROWS), slice(512, 640))] = jnp.where(edge > 0.0, both, 0.0)
        for move in moves[4:6]:
            move.wait()
        for f, (ref, index) in enumerate(fields):
            for k in range(layers):
                rows = slice(HALO * k, HALO * (k + 1))
                after = recv_x[1, slot + f, rows, :] * has_next_x
                before = recv_x[0, slot + f, rows, :] * has_prev_x
                ref[index + (k, slice(16, 16 + HALO), slice(0, 512))] = after
                ref[index + (k, slice(ROWS - HALO, ROWS), slice(0, 512))] = before

    loads[1].wait()
    loads[2].wait()

    def convert(k, carry):
        soil[k, 0:16, 0:512] = soil_ref[k].astype(jnp.float32)
        return carry

    lax.fori_loop(0, layers, convert, 0)

    pl.semaphore_wait(barrier, devices - 1)

    def scatter(x, y):
        pltpu.make_async_remote_copy(
            src_ref=send_c.at[x * size_y + y],
            dst_ref=recv_c.at[pl.ds(pl.multiple_of(me * 8, 8), 8)],
            send_sem=sem_c.at[0],
            recv_sem=sem_c.at[1],
            device_id=(x, y),
            device_id_type=MESH,
        ).start()

    others(scatter)
    opening = [(head, ()), (soil, ())]
    moves = start(0, 0, opening)

    def look_up(rows, lanes):
        def layer(k, carry):
            kind = soil[k, rows, lanes]
            values = [jnp.zeros(kind.shape, jnp.float32) for _ in range(3)]
            for c in range(table_ref.shape[1]):
                match = kind == float(c)
                values = [jnp.where(match, table_ref[p, c], v) for p, v in enumerate(values)]
            ksat[k, rows, lanes] = values[0] * mask[rows, lanes]
            steep[k, rows, lanes] = values[1]
            cap[k, rows, lanes] = values[2]
            return carry

        lax.fori_loop(0, layers, layer, 0)

    look_up(slice(0, 16), slice(0, 512))

    loads[3].wait()
    within = lax.broadcasted_iota(jnp.int32, (256, 512), 0)

    def spot(x, carry):
        slot = jnp.maximum(slot_ref[pl.ds(x, 1), :], 0)
        hot[x] = jnp.where(within == (slot & 255), 1.0, 0.0).astype(jnp.bfloat16)
        return carry

    lax.fori_loop(0, 16, spot, 0)

    finish(moves, 0, opening)
    look_up(slice(16, 24), slice(0, 512))
    look_up(slice(0, 24), slice(512, 640))

    def saturate(first):
        def layer(k, carry):
            a, ks, c = steep[k], ksat[k], cap[k]
            s = logistic(a * head[k])
            rise = a * s * (1.0 - s)
            conduct[k] = ks * (0.1 + 0.9 * s * s)
            slope[k] = 0.9 * ks * s * rise
            coef[0, k] = STORAGE * c * rise
            theta = (c * s)[0:16, 0:512]
            if first:
                wet[k] = s[0:16, 0:512]
                theta_old[k] = theta
            else:
                basis[0, k, 0:16, 0:512] = STORAGE * (theta - theta_old[k]) - source[k]
            return carry

        lax.fori_loop(0, layers, layer, 0, unroll=2)

    def saturate_again():
        def layer(k, carry):
            a, ks = steep[k], ksat[k]
            s = logistic(a * head[k])
            rise = a * s * (1.0 - s)
            conduct[k] = ks * (0.1 + 0.9 * s * s)
            slope[k] = 0.9 * ks * s * rise
            coef[0, k] = STORAGE * cap[k] * rise
            return carry

        lax.fori_loop(0, layers, layer, 0, unroll=2)

    def around(k):
        return jnp.minimum(k + 1, layers - 1), jnp.maximum(k - 1, 0)

    def balance():
        def layer(k, carry):
            h, kk = head[k], conduct[k]
            total = basis[0, k, 0:16, 0:512]
            for axis in range(2):
                flow = 0.5 * (kk + ahead(kk, axis)) * (h - ahead(h, axis))
                total = total + (flow - behind(flow, axis))[0:16, 0:512]
            below, above = around(k)
            h, kk = own(head, k), own(conduct, k)
            flow = 0.5 * (kk + own(conduct, below)) * (h - own(head, below) + 1.0)
            total = total + jnp.where(k == layers - 1, kk, flow)
            flow = 0.5 * (own(conduct, above) + kk) * (own(head, above) - h + 1.0)
            basis[0, k, 0:16, 0:512] = total - jnp.where(k == 0, 0.0, flow)
            return carry

        lax.fori_loop(0, layers, layer, 0, unroll=2)

    def linearize():
        scaled = mask[...] * (1.0 / SCALE)

        def layer(k, carry):
            h, kk, dk = head[k], conduct[k], slope[k]
            diagonal = coef[0, k] - SHIFT
            for axis, at in ((0, 1), (1, 3)):
                drop = h - ahead(h, axis)
                mean = 0.5 * (kk + ahead(kk, axis))
                mine = dk * drop + mean
                other = ahead(dk, axis) * drop - mean
                diagonal = diagonal + mine - behind(other, axis)
                coef[at, k] = other * scaled
                coef[at + 1, k] = -behind(mine, axis) * scaled
            below, above = around(k)
            bottom, top = k == layers - 1, k == 0
            drop = h - head[below] + 1.0
            mean = 0.5 * (kk + conduct[below])
            diagonal = diagonal + jnp.where(bottom, 2.0 * dk, dk * drop + mean)
            coef[5, k] = jnp.where(bottom, 0.0, slope[below] * drop - mean) * scaled
            drop = head[above] - h + 1.0
            mean = 0.5 * (kk + conduct[above])
            diagonal = diagonal - jnp.where(top, 0.0, dk * drop - mean)
            coef[6, k] = -jnp.where(top, 0.0, slope[above] * drop + mean) * scaled
            coef[0, k] = diagonal * scaled
            return carry

        lax.fori_loop(0, layers, layer, 0)

    saturate(True)
    linearize()

    def nothing(k, carry):
        basis[0, k, 0:16, 0:512] = jnp.zeros((16, 512), jnp.float32)
        return carry

    lax.fori_loop(0, layers, nothing, 0)
    balance()

    everything = pltpu.make_async_copy(
        recv_c.at[pl.ds(0, 8 * (devices - 1))], recv_c.at[pl.ds(0, 8 * (devices - 1))], sem_c.at[1]
    )
    everything.wait()
    blocks = devices // 4
    low = lax.broadcasted_iota(jnp.int32, (blocks, 128), 1) < CAP

    def put(r, left, right):
        value = jnp.concatenate([left, right], axis=1)
        high = value.astype(jnp.bfloat16)
        split[blocks * r : blocks * (r + 1), 0:256] = high
        split[blocks * r : blocks * (r + 1), 256:512] = (value - high.astype(jnp.float32)).astype(
            jnp.bfloat16
        )

    for r in range(8):
        plain = [recv_c[pl.ds(8 * c + r, blocks, stride=32), :] for c in range(4)]
        moved = [pltpu.roll(x, CAP, 1) for x in plain]
        put(r, jnp.where(low, plain[0], moved[1]), jnp.where(low, plain[2], moved[3]))
        if r >= 3:
            put(r + 5, jnp.where(low, moved[0], plain[1]), jnp.where(low, moved[2], plain[3]))

    which = lax.broadcasted_iota(jnp.int32, (blocks, 512), 0)

    def select(x, carry):
        slot = jnp.maximum(slot_ref[pl.ds(x, 1), :], 0)
        found = jnp.dot(
            split[...], jnp.concatenate([hot[x], hot[x]], axis=0), preferred_element_type=jnp.float32
        )
        match = which == (slot >> 8)
        for r in range(13):
            piece = jnp.where(match, found[blocks * r : blocks * (r + 1)], 0.0)
            records[r, pl.ds(x, 1), :] = jnp.sum(piece, axis=0, keepdims=True)
        return carry

    lax.fori_loop(0, 16, select, 0, unroll=2)
    loads[4].wait()

    sunlight, air, humidity, rainfall = (forcing_ref[i] for i in range(4))
    leaf, albedo, resist = (records[i] for i in range(3))
    total, roots = jnp.zeros_like(leaf), jnp.zeros_like(leaf)
    for k in range(layers):
        total = total + records[3 + k] * wet[k]
        roots = roots + records[3 + k]
    conductance = total / roots * leaf / (leaf + resist)
    exchange_coef = 0.5 + 0.3 * leaf
    radiation = (1.0 - albedo) * sunlight + 0.3
    surface = air
    for _ in range(2):
        vapour = 0.5 * jnp.exp(2.0 * (surface - air))
        square = surface * surface
        excess = (
            radiation
            - 0.3 * square * square
            - exchange_coef * (surface - air)
            - conductance * (vapour - humidity)
        )
        tangent = -1.2 * square * surface - exchange_coef - 2.0 * conductance * vapour
        surface = surface - excess / tangent
    evaporation = conductance * (0.5 * jnp.exp(2.0 * (surface - air)) - humidity)
    ks_top = own(ksat, 0)
    infiltration = rainfall * ks_top / (rainfall + ks_top)
    land = slot_ref[...] >= 0
    evaporation = jnp.where(land, evaporation, 0.0)
    infiltration = jnp.where(land, infiltration, 0.0)
    flux_ref[0] = evaporation
    flux_ref[1] = infiltration
    share = evaporation / total
    for k in range(layers):
        gain = -jnp.where(land, share * records[3 + k] * wet[k], 0.0)
        if k == 0:
            gain = gain + infiltration
        source[k] = gain
        basis[0, k, 0:16, 0:512] -= gain

    def fold(product):
        tall = product[0:8] + product[8:16]
        return (tall[:, 0:128] + tall[:, 128:256]) + (tall[:, 256:384] + tall[:, 384:512])

    lane1 = lax.broadcasted_iota(jnp.int32, (1, 128), 1)

    def place(partial, at, sums):
        for i, value in enumerate(sums):
            line = jnp.sum(value, axis=0, keepdims=True)
            partial = jnp.where(lane1 == at + i, jnp.sum(line, axis=1, keepdims=True), partial)
        return partial

    def matvec(j):
        rows, lanes = (slice(0, ROWS), slice(0, LANES)) if j + 1 < KRYLOV else (slice(0, 16), slice(0, 512))

        def layer(k, carry):
            v = basis[j, k]
            below, above = around(k)

            def term(i, value):
                return coef[i, k, rows, lanes] * value[rows, lanes]

            w = term(0, v)
            w = w + term(1, ahead(v, 0)) + term(2, behind(v, 0))
            w = w + term(3, ahead(v, 1)) + term(4, behind(v, 1))
            w = w + coef[5, k, rows, lanes] * basis[j, below, rows, lanes]
            w = w + coef[6, k, rows, lanes] * basis[j, above, rows, lanes]
            if j + 1 < KRYLOV:
                basis[j + 1, k] = w
            mine = w[0:16, 0:512]
            sums = [fold(mine * basis[i, k, 0:16, 0:512]) for i in range(j + 1)]
            sums.append(fold(mine * mine))
            return tuple(a + b for a, b in zip(carry, sums))

        zeros = tuple(jnp.zeros((8, 128), jnp.float32) for _ in range(j + 2))
        return lax.fori_loop(0, layers, layer, zeros, unroll=2)

    def square_of_start():
        def layer(k, carry):
            value = basis[0, k, 0:16, 0:512]
            return carry + fold(value * value)

        return [lax.fori_loop(0, layers, layer, jnp.zeros((8, 128), jnp.float32))]

    def reduce_all(n, partial):
        def along(stage, value, gather, sem, here, size, target):
            mine = part.at[n, stage]
            mine[...] = value
            gather[n, here] = value
            for i in range(1, size):
                pltpu.make_async_remote_copy(
                    src_ref=mine,
                    dst_ref=gather.at[n, here],
                    send_sem=sem.at[0, n],
                    recv_sem=sem.at[1, n],
                    device_id=target(lax.rem(here + i, size)),
                    device_id_type=MESH,
                ).start()
            rest = gather.at[n, pl.ds(0, size - 1)]
            pltpu.make_async_copy(rest, rest, sem.at[1, n]).wait()
            total = gather[n, 0]
            for i in range(1, size):
                total = total + gather[n, i]
            return total

        partial = along(0, partial, gather_x, sem_gx, gx, size_x, lambda d: (d, gy))
        return along(1, partial, gather_y, sem_gy, gy, size_y, lambda d: (gx, d))

    for n in range(NEWTON):
        field = [(basis, (0,))]
        moves = start(1 + n, 2 + n, field)
        partial = place(jnp.zeros((1, 128), jnp.float32), 0, square_of_start())
        if n:
            finish(head_moves, 4, [(head, ())])
            saturate_again()
            linearize()
        finish(moves, 2 + n, field)
        for j, at in ((0, 1), (1, 3), (2, 6)):
            partial = place(partial, at, matvec(j))
        sums = reduce_all(n, partial)
        gram = [[None] * 4 for _ in range(4)]
        at = 0
        for i in range(4):
            for j in range(i + 1):
                gram[i][j] = gram[j][i] = jnp.broadcast_to(sums[:, at : at + 1], (1, 128))
                at += 1
        weights = [w[:, 0:1] for w in krylov_weights(gram)]
        last = n + 1 == NEWTON
        rows, lanes = (slice(0, 16), slice(0, 512)) if last else (slice(0, ROWS), slice(0, LANES))

        def update(k, carry):
            value = head[k, rows, lanes]
            for i in range(KRYLOV):
                value = value - weights[i] * basis[i, k, rows, lanes]
            if last:
                out_ref[k] = value
            else:
                head[k] = value
            return carry

        lax.fori_loop(0, layers, update, 0)
        if not last:
            head_moves = start(3, 4, [(head, ())])
            saturate(False)
            balance()

    sent = send_c.at[pl.ds(0, devices - 1)]
    pltpu.make_async_copy(sent, sent, sem_c.at[0]).wait()
    for n in range(NEWTON):
        sent = gather_x.at[n, pl.ds(0, size_x - 1)]
        pltpu.make_async_copy(sent, sent, sem_gx.at[0, n]).wait()
        sent = gather_y.at[n, pl.ds(0, size_y - 1)]
        pltpu.make_async_copy(sent, sent, sem_gy.at[0, n]).wait()


def shards(sizes, head_old, soil_type, soil_table, forcing, canopy, column_slot):
    layers = head_old.shape[0]
    devices = sizes[0] * sizes[1]
    f32 = jnp.float32
    wide = (layers, ROWS, LANES)
    tile = (layers, 16, 512)
    vmem, anywhere = pl.BlockSpec(memory_space=pltpu.VMEM), pl.BlockSpec(memory_space=pl.ANY)
    return pl.pallas_call(
        functools.partial(kernel, sizes),
        out_shape=(
            jax.ShapeDtypeStruct(head_old.shape, f32),
            jax.ShapeDtypeStruct((2, 16, 512), f32),
        ),
        in_specs=[anywhere, anywhere, pl.BlockSpec(memory_space=pltpu.SMEM)] + [anywhere] * 3,
        out_specs=(vmem, vmem),
        scratch_shapes=[
            pltpu.VMEM(tile, jnp.int32),
            pltpu.VMEM(forcing.shape, f32),
            pltpu.VMEM(canopy.shape, f32),
            pltpu.VMEM(column_slot.shape, jnp.int32),
            pltpu.VMEM((devices, 8, 128), f32),
            pltpu.VMEM((devices * 8, 128), f32),
            pltpu.VMEM((13 * (devices // 4), 512), jnp.bfloat16),
            pltpu.VMEM((16, 256, 512), jnp.bfloat16),
            pltpu.VMEM((13, 16, 512), f32),
            pltpu.VMEM(wide, f32),
            pltpu.VMEM(wide, f32),
            pltpu.VMEM(wide, f32),
            pltpu.VMEM(wide, f32),
            pltpu.VMEM(wide, f32),
            pltpu.VMEM(wide, f32),
            pltpu.VMEM(wide, f32),
            pltpu.VMEM((7,) + wide, f32),
            pltpu.VMEM((KRYLOV,) + wide, f32),
            pltpu.VMEM(tile, f32),
            pltpu.VMEM(tile, f32),
            pltpu.VMEM(tile, f32),
            pltpu.VMEM((ROWS, LANES), f32),
            pltpu.VMEM((2, 5, 32, 512), f32),
            pltpu.VMEM((2, 5, 32, 512), f32),
            pltpu.VMEM((2, 5, 16, 128), f32),
            pltpu.VMEM((2, 5, 16, 128), f32),
            pltpu.VMEM((2, 2, 5, 8, 128), f32),
            pltpu.VMEM((NEWTON, 2, 1, 128), f32),
            pltpu.VMEM((NEWTON, sizes[0], 1, 128), f32),
            pltpu.VMEM((NEWTON, sizes[1], 1, 128), f32),
            pltpu.SemaphoreType.DMA((5,)),
            pltpu.SemaphoreType.DMA((2,)),
            pltpu.SemaphoreType.DMA((2, 4, 8)),
            pltpu.SemaphoreType.DMA((2, NEWTON)),
            pltpu.SemaphoreType.DMA((2, NEWTON)),
        ],
        compiler_params=pltpu.CompilerParams(collective_id=0, has_side_effects=True),
        name="coupled_step",
    )(head_old, soil_type, soil_table, forcing, canopy, column_slot)


def solution(mesh):
    sizes = (mesh.shape["gx"], mesh.shape["gy"])
    return jax.shard_map(
        functools.partial(shards, sizes),
        mesh=mesh,
        in_specs=(
            P(None, "gx", "gy"),
            P(None, "gx", "gy"),
            P(),
            P(None, "gx", "gy"),
            P(None, ("gx", "gy")),
            P("gx", "gy"),
        ),
        out_specs=(P(None, "gx", "gy"), P(None, "gx", "gy")),
        check_vma=False,
    )
```

time: 94.5 us -> 71.9 us (0.76)
  Pallas kernels: 91.4 us -> 68.7 us
    pallas_call x1, Pallas kernels: 91.4 us -> 68.7 us  [shards(): pl.pallas_call(functools.partial(kernel, sizes), out_shape=(jax.ShapeDtyp...]
where the time goes in v2:
time: 71.9 us; the launch traced here: 71.7 us
  Pallas kernels  68.7 us (96%)
  local copies, waits for them, and re-layouts  2.38 us (3%)
    pallas_call x1, Pallas kernels, shards(): pl.pallas_call(functools.partial(kernel, sizes), out_shape=(jax.ShapeDtyp...  68.7 us
    unnamed x4, local copies, waits for them, and re-layouts  2.38 us

profile of v2, /device:TPU:1, one launch (start us, length us, event | category | flops | bytes accessed | tf_op | source)
XLA Modules:
  0.0 71.7 jit_solution(3473253332929575156)
XLA Ops:
  0.6 68.7 %coupled_step.1 = (f32[10,16,512]{2,1,0:T(8,128)}, f32[2,16,512]{2,1,0:T(8,128)}) custom-call(f32[10,16,512]{2,1,0:T(8,128)} %head_in.1, s32[10,16,512]{2,1,0:T(8,128)} %soil_in.1, f32[3,12]{1,0:T(4,128)} %table_ref.1, f32[4,16,512]{2,1,0:T(8,128)} %forcing_in.1, f32[13,8192]{1,0:T(8,128)} %canopy_in.1, s32[16,512]{1,0:T(8,128)} %slot_in.1), custom_call_target="tpu_custom_call" | custom-call | tf_op jit(solution)/shard_map/coupled_step/pallas_call | solution.py:654
  69.3 0.0 copy-start
  69.3 1.7 %copy.10 = f32[10,16,512]{2,1,0:T(8,128)} copy(f32[10,16,512]{2,1,0:T(8,128)} %get-tuple-element.4) | data formatting | bytes 655360
  71.1 0.0 copy-done
  71.1 0.6 copy.11
Async XLA Ops:
  69.3 1.8 %copy-start = (f32[2,16,512]{2,1,0:T(8,128)S(1)}, f32[2,16,512]{2,1,0:T(8,128)}, u32[]{:S(2)}) copy-start(f32[2,16,512]{2,1,0:T(8,128)} %get-tuple-element.5) | copy-start | bytes 196612

commit v3 on v2

--- a/solution.py
+++ b/solution.py
@@ -18,6 +18,8 @@
 SCALE = 3.0
 
 MESH = pl.DeviceIdType.MESH
+OWN = (slice(0, 16), slice(0, 512))
+RIM = ((slice(16, 24), slice(0, 512)), (slice(0, 24), slice(512, 640)))
 HALO = 3
 ROWS = 24
 LANES = 640
@@ -102,12 +104,13 @@
     sizes,
     head_in,
     soil_in,
-    table_ref,
+    table_in,
     forcing_in,
     canopy_in,
     slot_in,
     out_ref,
     flux_ref,
+    table_ref,
     soil_ref,
     forcing_ref,
     canopy_ref,
@@ -159,6 +162,7 @@
                 (soil_in, soil_ref),
                 (slot_in, slot_ref),
                 (forcing_in, forcing_ref),
+                (table_in, table_ref),
             )
         )
     ]
@@ -217,19 +221,26 @@
         for slot in range(5):
             send_x[side, slot, 24:32, :] = jnp.zeros((8, 512), jnp.float32)
 
-    lane8 = lax.broadcasted_iota(jnp.int32, (8, 128), 1)
-    low8 = lane8 < CAP
+    low7 = lax.broadcasted_iota(jnp.int32, (7, 128), 1) < CAP
 
     def pack(q, carry):
         lanes = pl.ds(pl.multiple_of(q * 128, 128), 128)
-        first, second = canopy_ref[0:8, lanes], canopy_ref[5:13, lanes]
-        send_c[2 * q] = jnp.where(low8, first, pltpu.roll(second, CAP, 1))
-        send_c[2 * q + 1] = jnp.where(low8, pltpu.roll(first, CAP, 1), second)
+        first, second = canopy_ref[0:7, lanes], canopy_ref[6:13, lanes]
+        send_c[2 * q, 0:7] = jnp.where(low7, first, pltpu.roll(second, CAP, 1))
+        send_c[2 * q + 1, 0:7] = jnp.where(low7, pltpu.roll(first, CAP, 1), second)
         return carry
 
     loads[0].wait()
     lax.fori_loop(0, devices // 2, pack, 0, unroll=4)
-    recv_c[pl.ds(pl.multiple_of(me * 8, 8), 8), :] = send_c[me]
+    quarter = size_x // 4
+
+    def seat(x):
+        return lax.rem(gx - x + quarter + size_x, size_x)
+
+    def slab(x):
+        return pl.ds(pl.multiple_of((seat(x) * size_y + gy) * 8, 8), 7)
+
+    recv_c[slab(gx), :] = send_c[me, 0:7]
 
     next_x, prev_x = wrap(gx + 1, size_x), wrap(gx - 1, size_x)
     next_y, prev_y = wrap(gy + 1, size_y), wrap(gy - 1, size_y)
@@ -323,17 +334,17 @@
 
     def scatter(x, y):
         pltpu.make_async_remote_copy(
-            src_ref=send_c.at[x * size_y + y],
-            dst_ref=recv_c.at[pl.ds(pl.multiple_of(me * 8, 8), 8)],
+            src_ref=send_c.at[x * size_y + y, pl.ds(0, 7)],
+            dst_ref=recv_c.at[slab(x)],
             send_sem=sem_c.at[0],
-            recv_sem=sem_c.at[1],
+            recv_sem=sem_c.at[1 + seat(x) // (size_x // 2)],
             device_id=(x, y),
             device_id_type=MESH,
         ).start()
 
-    others(scatter)
     opening = [(head, ()), (soil, ())]
     moves = start(0, 0, opening)
+    others(scatter)
 
     def look_up(rows, lanes):
         def layer(k, carry):
@@ -349,51 +360,92 @@
 
         lax.fori_loop(0, layers, layer, 0)
 
-    look_up(slice(0, 16), slice(0, 512))
+    loads[5].wait()
+    look_up(*OWN)
+
+    def saturate(rows, lanes, keep):
+        def layer(k, carry):
+            a, ks, c = (ref[k, rows, lanes] for ref in (steep, ksat, cap))
+            s = logistic(a * head[k, rows, lanes])
+            rise = a * s * (1.0 - s)
+            conduct[k, rows, lanes] = ks * (0.1 + 0.9 * s * s)
+            slope[k, rows, lanes] = 0.9 * ks * s * rise
+            coef[0, k, rows, lanes] = STORAGE * c * rise
+            keep(k, s, c)
+            return carry
+
+        lax.fori_loop(0, layers, layer, 0, unroll=2)
+
+    def keep_old(k, s, c):
+        wet[k] = s
+        theta_old[k] = c * s
+
+    def keep_residual(k, s, c):
+        basis[0, k, 0:16, 0:512] = STORAGE * (c * s - theta_old[k]) - source[k]
+
+    def keep_none(k, s, c):
+        pass
+
+    saturate(*OWN, keep_old)
 
     loads[3].wait()
     within = lax.broadcasted_iota(jnp.int32, (256, 512), 0)
 
+    def seats_of(x):
+        slot = jnp.maximum(slot_ref[pl.ds(x, 1), :], 0)
+        shift = (size_y * CAP).bit_length() - 1
+        seat = ((slot >> shift) - gx + quarter) & (size_x - 1)
+        return (seat << shift) + (slot & (size_y * CAP - 1))
+
     def spot(x, carry):
-        slot = jnp.maximum(slot_ref[pl.ds(x, 1), :], 0)
+        slot = seats_of(x)
         hot[x] = jnp.where(within == (slot & 255), 1.0, 0.0).astype(jnp.bfloat16)
         return carry
 
     lax.fori_loop(0, 16, spot, 0)
 
+    blocks = devices // 8
+    low = lax.broadcasted_iota(jnp.int32, (blocks, 128), 1) < CAP
+    which = lax.broadcasted_iota(jnp.int32, (blocks, 512), 0)
+
+    def choose(part_of):
+        arrived = send_c.at[pl.ds(0, devices // 2 - (1 - part_of)), pl.ds(0, 7)]
+        pltpu.make_async_copy(arrived, arrived, sem_c.at[1 + part_of]).wait()
+
+        def put(r, left, right):
+            value = jnp.concatenate([left, right], axis=1)
+            high = value.astype(jnp.bfloat16)
+            rows = slice(blocks * r, blocks * (r + 1))
+            split[rows, 0:256] = high
+            split[rows, 256:512] = (value - high.astype(jnp.float32)).astype(jnp.bfloat16)
+
+        for r in range(7):
+            first = 32 * blocks * part_of + r
+            plain = [recv_c[pl.ds(first + 8 * c, blocks, stride=32), :] for c in range(4)]
+            moved = [pltpu.roll(x, CAP, 1) for x in plain]
+            put(r, jnp.where(low, plain[0], moved[1]), jnp.where(low, plain[2], moved[3]))
+            if r >= 1:
+                put(r + 6, jnp.where(low, moved[0], plain[1]), jnp.where(low, moved[2], plain[3]))
+
+        def select(x, carry):
+            found = jnp.dot(
+                split[...], jnp.concatenate([hot[x], hot[x]], axis=0), preferred_element_type=jnp.float32
+            )
+            match = which == (seats_of(x) >> 8) - blocks * part_of
+            for r in range(13):
+                piece = jnp.where(match, found[blocks * r : blocks * (r + 1)], 0.0)
+                value = jnp.sum(piece, axis=0, keepdims=True)
+                if part_of:
+                    value = value + records[r, pl.ds(x, 1), :]
+                records[r, pl.ds(x, 1), :] = value
+            return carry
+
+        lax.fori_loop(0, 16, select, 0, unroll=2)
+
+    choose(0)
     finish(moves, 0, opening)
-    look_up(slice(16, 24), slice(0, 512))
-    look_up(slice(0, 24), slice(512, 640))
-
-    def saturate(first):
-        def layer(k, carry):
-            a, ks, c = steep[k], ksat[k], cap[k]
-            s = logistic(a * head[k])
-            rise = a * s * (1.0 - s)
-            conduct[k] = ks * (0.1 + 0.9 * s * s)
-            slope[k] = 0.9 * ks * s * rise
-            coef[0, k] = STORAGE * c * rise
-            theta = (c * s)[0:16, 0:512]
-            if first:
-                wet[k] = s[0:16, 0:512]
-                theta_old[k] = theta
-            else:
-                basis[0, k, 0:16, 0:512] = STORAGE * (theta - theta_old[k]) - source[k]
-            return carry
-
-        lax.fori_loop(0, layers, layer, 0, unroll=2)
-
-    def saturate_again():
-        def layer(k, carry):
-            a, ks = steep[k], ksat[k]
-            s = logistic(a * head[k])
-            rise = a * s * (1.0 - s)
-            conduct[k] = ks * (0.1 + 0.9 * s * s)
-            slope[k] = 0.9 * ks * s * rise
-            coef[0, k] = STORAGE * cap[k] * rise
-            return carry
-
-        lax.fori_loop(0, layers, layer, 0, unroll=2)
+    for region in RIM:
+        look_up(*region)
 
     def around(k):
         return jnp.minimum(k + 1, layers - 1), jnp.maximum(k - 1, 0)
@@ -415,83 +467,59 @@
 
         lax.fori_loop(0, layers, layer, 0, unroll=2)
 
-    def linearize():
-        scaled = mask[...] * (1.0 / SCALE)
+    def linearize(rows, lanes, flows=False):
+        def at(x):
+            return x[rows, lanes]
 
         def layer(k, carry):
+            scaled = mask[rows, lanes] * (1.0 / SCALE)
             h, kk, dk = head[k], conduct[k], slope[k]
-            diagonal = coef[0, k] - SHIFT
-            for axis, at in ((0, 1), (1, 3)):
+            diagonal = coef[0, k, rows, lanes] - SHIFT
+            total = None
+            for axis, i in ((0, 1), (1, 3)):
                 drop = h - ahead(h, axis)
                 mean = 0.5 * (kk + ahead(kk, axis))
                 mine = dk * drop + mean
                 other = ahead(dk, axis) * drop - mean
-                diagonal = diagonal + mine - behind(other, axis)
-                coef[at, k] = other * scaled
-                coef[at + 1, k] = -behind(mine, axis) * scaled
+                diagonal = diagonal + at(mine) - at(behind(other, axis))
+                coef[i, k, rows, lanes] = at(other) * scaled
+                coef[i + 1, k, rows, lanes] = -at(behind(mine, axis)) * scaled
+                if flows:
+                    flow = mean * drop
+                    net = at(flow) - at(behind(flow, axis))
+                    total = net if total is None else total + net
             below, above = around(k)
             bottom, top = k == layers - 1, k == 0
-            drop = h - head[below] + 1.0
-            mean = 0.5 * (kk + conduct[below])
+            h, kk, dk = at(h), at(kk), at(dk)
+            drop = h - head[below, rows, lanes] + 1.0
+            mean = 0.5 * (kk + conduct[below, rows, lanes])
             diagonal = diagonal + jnp.where(bottom, 2.0 * dk, dk * drop + mean)
-            coef[5, k] = jnp.where(bottom, 0.0, slope[below] * drop - mean) * scaled
-            drop = head[above] - h + 1.0
-            mean = 0.5 * (kk + conduct[above])
+            coef[5, k, rows, lanes] = (
+                jnp.where(bottom, 0.0, slope[below, rows, lanes] * drop - mean) * scaled
+            )
+            if flows:
+                total = total + jnp.where(bottom, kk, mean * drop)
+            drop = head[above, rows, lanes] - h + 1.0
+            mean = 0.5 * (kk + conduct[above, rows, lanes])
             diagonal = diagonal - jnp.where(top, 0.0, dk * drop - mean)
-            coef[6, k] = -jnp.where(top, 0.0, slope[above] * drop + mean) * scaled
-            coef[0, k] = diagonal * scaled
+            coef[6, k, rows, lanes] = (
+                -jnp.where(top, 0.0, slope[above, rows, lanes] * drop + mean) * scaled
+            )
+            if flows:
+                basis[0, k, rows, lanes] = total - jnp.where(top, 0.0, mean * drop)
+            coef[0, k, rows, lanes] = diagonal * scaled
             return carry
 
         lax.fori_loop(0, layers, layer, 0)
 
-    saturate(True)
-    linearize()
-
-    def nothing(k, carry):
-        basis[0, k, 0:16, 0:512] = jnp.zeros((16, 512), jnp.float32)
-        return carry
-
-    lax.fori_loop(0, layers, nothing, 0)
-    balance()
-
-    everything = pltpu.make_async_copy(
-        recv_c.at[pl.ds(0, 8 * (devices - 1))], recv_c.at[pl.ds(0, 8 * (devices - 1))], sem_c.at[1]
-    )
-    everything.wait()
-    blocks = devices // 4
-    low = lax.broadcasted_iota(jnp.int32, (blocks, 128), 1) < CAP
-
-    def put(r, left, right):
-        value = jnp.concatenate([left, right], axis=1)
-        high = value.astype(jnp.bfloat16)
-        split[blocks * r : blocks * (r + 1), 0:256] = high
-        split[blocks * r : blocks * (r + 1), 256:512] = (value - high.astype(jnp.float32)).astype(
-            jnp.bfloat16
-        )
-
-    for r in range(8):
-        plain = [recv_c[pl.ds(8 * c + r, blocks, stride=32), :] for c in range(4)]
-        moved = [pltpu.roll(x, CAP, 1) for x in plain]
-        put(r, jnp.where(low, plain[0], moved[1]), jnp.where(low, plain[2], moved[3]))
-        if r >= 3:
-            put(r + 5, jnp.where(low, moved[0], plain[1]), jnp.where(low, moved[2], plain[3]))
-
-    which = lax.broadcasted_iota(jnp.int32, (blocks, 512), 0)
-
-    def select(x, carry):
-        slot = jnp.maximum(slot_ref[pl.ds(x, 1), :], 0)
-        found = jnp.dot(
-            split[...], jnp.concatenate([hot[x], hot[x]], axis=0), preferred_element_type=jnp.float32
-        )
-        match = which == (slot >> 8)
-        for r in range(13):
-            piece = jnp.where(match, found[blocks * r : blocks * (r + 1)], 0.0)
-            records[r, pl.ds(x, 1), :] = jnp.sum(piece, axis=0, keepdims=True)
-        return carry
-
-    lax.fori_loop(0, 16, select, 0, unroll=2)
+    for region in RIM:
+        saturate(*region, keep_none)
+    linearize(*OWN, flows=True)
+    for region in RIM:
+        linearize(*region)
+
+    choose(1)
     loads[4].wait()
-
     sunlight, air, humidity, rainfall = (forcing_ref[i] for i in range(4))
     leaf, albedo, resist = (records[i] for i in range(3))
     total, roots = jnp.zeros_like(leaf), jnp.zeros_like(leaf)
@@ -602,9 +630,12 @@
         moves = start(1 + n, 2 + n, field)
         partial = place(jnp.zeros((1, 128), jnp.float32), 0, square_of_start())
         if n:
+            linearize(*OWN)
             finish(head_moves, 4, [(head, ())])
-            saturate_again()
-            linearize()
+            for region in RIM:
+                saturate(*region, keep_none)
+            for region in RIM:
+                linearize(*region)
         finish(moves, 2 + n, field)
         for j, at in ((0, 1), (1, 3), (2, 6)):
             partial = place(partial, at, matvec(j))
@@ -632,10 +663,12 @@
         lax.fori_loop(0, layers, update, 0)
         if not last:
             head_moves = start(3, 4, [(head, ())])
-            saturate(False)
+            saturate(*OWN, keep_residual)
+            for region in RIM:
+                saturate(*region, keep_none)
             balance()
 
-    sent = send_c.at[pl.ds(0, devices - 1)]
+    sent = send_c.at[pl.ds(0, devices - 1), pl.ds(0, 7)]
     pltpu.make_async_copy(sent, sent, sem_c.at[0]).wait()
     for n in range(NEWTON):
         sent = gather_x.at[n, pl.ds(0, size_x - 1)]
@@ -650,23 +683,24 @@
     f32 = jnp.float32
     wide = (layers, ROWS, LANES)
     tile = (layers, 16, 512)
-    vmem, anywhere = pl.BlockSpec(memory_space=pltpu.VMEM), pl.BlockSpec(memory_space=pl.ANY)
+    vmem, hbm = pl.BlockSpec(memory_space=pltpu.VMEM), pl.BlockSpec(memory_space=pltpu.HBM)
     return pl.pallas_call(
         functools.partial(kernel, sizes),
         out_shape=(
             jax.ShapeDtypeStruct(head_old.shape, f32),
             jax.ShapeDtypeStruct((2, 16, 512), f32),
         ),
-        in_specs=[anywhere, anywhere, pl.BlockSpec(memory_space=pltpu.SMEM)] + [anywhere] * 3,
+        in_specs=[hbm] * 6,
         out_specs=(vmem, vmem),
         scratch_shapes=[
+            pltpu.SMEM(soil_table.shape, f32),
             pltpu.VMEM(tile, jnp.int32),
             pltpu.VMEM(forcing.shape, f32),
             pltpu.VMEM(canopy.shape, f32),
             pltpu.VMEM(column_slot.shape, jnp.int32),
             pltpu.VMEM((devices, 8, 128), f32),
             pltpu.VMEM((devices * 8, 128), f32),
-            pltpu.VMEM((13 * (devices // 4), 512), jnp.bfloat16),
+            pltpu.VMEM((13 * (devices // 8), 512), jnp.bfloat16),
             pltpu.VMEM((16, 256, 512), jnp.bfloat16),
             pltpu.VMEM((13, 16, 512), f32),
             pltpu.VMEM(wide, f32),
@@ -690,13 +724,15 @@
             pltpu.VMEM((NEWTON, 2, 1, 128), f32),
             pltpu.VMEM((NEWTON, sizes[0], 1, 128), f32),
             pltpu.VMEM((NEWTON, sizes[1], 1, 128), f32),
-            pltpu.SemaphoreType.DMA((5,)),
-            pltpu.SemaphoreType.DMA((2,)),
+            pltpu.SemaphoreType.DMA((6,)),
+            pltpu.SemaphoreType.DMA((3,)),
             pltpu.SemaphoreType.DMA((2, 4, 8)),
             pltpu.SemaphoreType.DMA((2, NEWTON)),
             pltpu.SemaphoreType.DMA((2, NEWTON)),
         ],
-        compiler_params=pltpu.CompilerParams(collective_id=0, has_side_effects=True),
+        compiler_params=pltpu.CompilerParams(
+            collective_id=0, has_side_effects=True, vmem_limit_bytes=40 * 1024 * 1024
+        ),
         name="coupled_step",
     )(head_old, soil_type, soil_table, forcing, canopy, column_slot)
 

time: 71.9 us -> 79.8 us (1.11)
  local copies, waits for them, and re-layouts: 2.38 us -> 6.68 us
  Pallas kernels: 68.7 us -> 72.1 us
    unnamed x4 -> x14, local copies, waits for them, and re-layouts: 2.38 us -> 6.68 us
    pallas_call x1, Pallas kernels: 68.7 us -> 72.1 us  [shards(): pl.pallas_call(functools.partial(kernel, sizes), out_shape=(jax.ShapeDtyp...]
where the time goes in v3:
time: 79.8 us; the launch traced here: 79.4 us
  Pallas kernels  72.1 us (90%)
  local copies, waits for them, and re-layouts  6.68 us (8%)
    pallas_call x1, Pallas kernels, shards(): pl.pallas_call(functools.partial(kernel, sizes), out_shape=(jax.ShapeDtyp...  72.1 us
    unnamed x14, local copies, waits for them, and re-layouts  6.68 us

profile of v3, /device:TPU:1, one launch (start us, length us, event | category | flops | bytes accessed | tf_op | source)
XLA Modules:
  0.0 79.4 jit_solution(2118369873765173741)
XLA Ops:
  0.6 0.0 copy-start
  0.6 1.0 %copy-done = f32[13,8192]{1,0:T(8,128)S(1)} copy-done((f32[13,8192]{1,0:T(8,128)S(1)}, f32[13,8192]{1,0:T(8,128)}, u32[]{:S(2)}) %copy-start) | copy-done | bytes 426008
  1.7 0.0 copy-start.1
  1.7 1.0 %copy-done.1 = f32[10,16,512]{2,1,0:T(8,128)S(1)} copy-done((f32[10,16,512]{2,1,0:T(8,128)S(1)}, f32[10,16,512]{2,1,0:T(8,128)}, u32[]{:S(2)}) %copy-start.1) | copy-done | bytes 327704
  2.6 0.0 copy-start.2
  2.6 1.0 %copy-done.2 = s32[10,16,512]{2,1,0:T(8,128)S(1)} copy-done((s32[10,16,512]{2,1,0:T(8,128)S(1)}, s32[10,16,512]{2,1,0:T(8,128)}, u32[]{:S(2)}) %copy-start.2) | copy-done | bytes 327704
  3.6 0.0 copy-start.3
  3.6 0.9 %copy-done.3 = f32[4,16,512]{2,1,0:T(8,128)S(1)} copy-done((f32[4,16,512]{2,1,0:T(8,128)S(1)}, f32[4,16,512]{2,1,0:T(8,128)}, u32[]{:S(2)}) %copy-start.3) | copy-done | bytes 131096
  4.5 0.0 copy-start.4
  4.5 0.8 copy-done.4
  5.3 0.0 copy-start.5
  5.3 0.7 copy-done.5
  6.0 72.1 %coupled_step.1 = (f32[10,16,512]{2,1,0:T(8,128)S(1)}, f32[2,16,512]{2,1,0:T(8,128)S(1)}) custom-call(f32[10,16,512]{2,1,0:T(8,128)S(1)} %copy-done.1, s32[10,16,512]{2,1,0:T(8,128)S(1)} %copy-done.2, f32[3,12]{1,0:T(4,128)S(1)} %copy-done.5, f32[4,16,512]{2,1,0:T(8,128)S(1)} %copy-done.3, f32[13,8192]{1,0:T(8,128)S(1)} %copy-done, s32[16,512]{1,0:T(8,128)S(1)} %copy-done.4), custom_call_target="tpu_custom_call" | custom-call | tf_op jit(solution)/shard_map/coupled_step/pallas_call | solution.py:687
  78.1 0.7 copy.10
  78.8 0.6 copy.11
Async XLA Ops:
  0.6 1.0 %copy-start = (f32[13,8192]{1,0:T(8,128)S(1)}, f32[13,8192]{1,0:T(8,128)}, u32[]{:S(2)}) copy-start(f32[13,8192]{1,0:T(8,128)} %canopy_in.1) | copy-start | bytes 1277956
  1.7 1.0 %copy-start.1 = (f32[10,16,512]{2,1,0:T(8,128)S(1)}, f32[10,16,512]{2,1,0:T(8,128)}, u32[]{:S(2)}) copy-start(f32[10,16,512]{2,1,0:T(8,128)} %head_in.1) | copy-start | bytes 983044
  2.6 1.0 %copy-start.2 = (s32[10,16,512]{2,1,0:T(8,128)S(1)}, s32[10,16,512]{2,1,0:T(8,128)}, u32[]{:S(2)}) copy-start(s32[10,16,512]{2,1,0:T(8,128)} %soil_in.1) | copy-start | bytes 983044
  3.6 0.9 %copy-start.3 = (f32[4,16,512]{2,1,0:T(8,128)S(1)}, f32[4,16,512]{2,1,0:T(8,128)}, u32[]{:S(2)}) copy-start(f32[4,16,512]{2,1,0:T(8,128)} %forcing_in.1) | copy-start | bytes 393220
  4.5 0.8 copy-start.4
  5.3 0.7 copy-start.5

commit v4 on v3

--- a/solution.py
+++ b/solution.py
@@ -337,7 +337,7 @@
             src_ref=send_c.at[x * size_y + y, pl.ds(0, 7)],
             dst_ref=recv_c.at[slab(x)],
             send_sem=sem_c.at[0],
-            recv_sem=sem_c.at[1 + seat(x) // (size_x // 2)],
+            recv_sem=sem_c.at[1],
             device_id=(x, y),
             device_id_type=MESH,
         ).start()
@@ -404,45 +404,6 @@
 
     lax.fori_loop(0, 16, spot, 0)
 
-    blocks = devices // 8
-    low = lax.broadcasted_iota(jnp.int32, (blocks, 128), 1) < CAP
-    which = lax.broadcasted_iota(jnp.int32, (blocks, 512), 0)
-
-    def choose(part_of):
-        arrived = send_c.at[pl.ds(0, devices // 2 - (1 - part_of)), pl.ds(0, 7)]
-        pltpu.make_async_copy(arrived, arrived, sem_c.at[1 + part_of]).wait()
-
-        def put(r, left, right):
-            value = jnp.concatenate([left, right], axis=1)
-            high = value.astype(jnp.bfloat16)
-            rows = slice(blocks * r, blocks * (r + 1))
-            split[rows, 0:256] = high
-            split[rows, 256:512] = (value - high.astype(jnp.float32)).astype(jnp.bfloat16)
-
-        for r in range(7):
-            first = 32 * blocks * part_of + r
-            plain = [recv_c[pl.ds(first + 8 * c, blocks, stride=32), :] for c in range(4)]
-            moved = [pltpu.roll(x, CAP, 1) for x in plain]
-            put(r, jnp.where(low, plain[0], moved[1]), jnp.where(low, plain[2], moved[3]))
-            if r >= 1:
-                put(r + 6, jnp.where(low, moved[0], plain[1]), jnp.where(low, moved[2], plain[3]))
-
-        def select(x, carry):
-            found = jnp.dot(
-                split[...], jnp.concatenate([hot[x], hot[x]], axis=0), preferred_element_type=jnp.float32
-            )
-            match = which == (seats_of(x) >> 8) - blocks * part_of
-            for r in range(13):
-                piece = jnp.where(match, found[blocks * r : blocks * (r + 1)], 0.0)
-                value = jnp.sum(piece, axis=0, keepdims=True)
-                if part_of:
-                    value = value + records[r, pl.ds(x, 1), :]
-                records[r, pl.ds(x, 1), :] = value
-            return carry
-
-        lax.fori_loop(0, 16, select, 0, unroll=2)
-
-    choose(0)
     finish(moves, 0, opening)
     for region in RIM:
         look_up(*region)
@@ -467,58 +428,83 @@
 
         lax.fori_loop(0, layers, layer, 0, unroll=2)
 
-    def linearize(rows, lanes, flows=False):
-        def at(x):
-            return x[rows, lanes]
-
+    def linearize(flows):
         def layer(k, carry):
-            scaled = mask[rows, lanes] * (1.0 / SCALE)
+            scaled = mask[...] * (1.0 / SCALE)
             h, kk, dk = head[k], conduct[k], slope[k]
-            diagonal = coef[0, k, rows, lanes] - SHIFT
+            diagonal = coef[0, k] - SHIFT
             total = None
-            for axis, i in ((0, 1), (1, 3)):
+            for axis, at in ((0, 1), (1, 3)):
                 drop = h - ahead(h, axis)
                 mean = 0.5 * (kk + ahead(kk, axis))
                 mine = dk * drop + mean
                 other = ahead(dk, axis) * drop - mean
-                diagonal = diagonal + at(mine) - at(behind(other, axis))
-                coef[i, k, rows, lanes] = at(other) * scaled
-                coef[i + 1, k, rows, lanes] = -at(behind(mine, axis)) * scaled
+                diagonal = diagonal + mine - behind(other, axis)
+                coef[at, k] = other * scaled
+                coef[at + 1, k] = -behind(mine, axis) * scaled
                 if flows:
                     flow = mean * drop
-                    net = at(flow) - at(behind(flow, axis))
+                    net = flow - behind(flow, axis)
                     total = net if total is None else total + net
             below, above = around(k)
             bottom, top = k == layers - 1, k == 0
-            h, kk, dk = at(h), at(kk), at(dk)
-            drop = h - head[below, rows, lanes] + 1.0
-            mean = 0.5 * (kk + conduct[below, rows, lanes])
+            drop = h - head[below] + 1.0
+            mean = 0.5 * (kk + conduct[below])
             diagonal = diagonal + jnp.where(bottom, 2.0 * dk, dk * drop + mean)
-            coef[5, k, rows, lanes] = (
-                jnp.where(bottom, 0.0, slope[below, rows, lanes] * drop - mean) * scaled
-            )
+            coef[5, k] = jnp.where(bottom, 0.0, slope[below] * drop - mean) * scaled
             if flows:
                 total = total + jnp.where(bottom, kk, mean * drop)
-            drop = head[above, rows, lanes] - h + 1.0
-            mean = 0.5 * (kk + conduct[above, rows, lanes])
+            drop = head[above] - h + 1.0
+            mean = 0.5 * (kk + conduct[above])
             diagonal = diagonal - jnp.where(top, 0.0, dk * drop - mean)
-            coef[6, k, rows, lanes] = (
-                -jnp.where(top, 0.0, slope[above, rows, lanes] * drop + mean) * scaled
-            )
+            coef[6, k] = -jnp.where(top, 0.0, slope[above] * drop + mean) * scaled
             if flows:
-                basis[0, k, rows, lanes] = total - jnp.where(top, 0.0, mean * drop)
-            coef[0, k, rows, lanes] = diagonal * scaled
+                total = total - jnp.where(top, 0.0, mean * drop)
+                basis[0, k, 0:16, 0:512] = total[0:16, 0:512]
+            coef[0, k] = diagonal * scaled
             return carry
 
         lax.fori_loop(0, layers, layer, 0)
 
     for region in RIM:
         saturate(*region, keep_none)
-    linearize(*OWN, flows=True)
-    for region in RIM:
-        linearize(*region)
-
-    choose(1)
+    linearize(True)
+
+    blocks = devices // 4
+    low = lax.broadcasted_iota(jnp.int32, (blocks, 128), 1) < CAP
+    which = lax.broadcasted_iota(jnp.int32, (blocks, 512), 0)
+
+    def choose():
+        arrived = send_c.at[pl.ds(0, devices - 1), pl.ds(0, 7)]
+        pltpu.make_async_copy(arrived, arrived, sem_c.at[1]).wait()
+
+        def put(r, left, right):
+            value = jnp.concatenate([left, right], axis=1)
+            high = value.astype(jnp.bfloat16)
+            rows = slice(blocks * r, blocks * (r + 1))
+            split[rows, 0:256] = high
+            split[rows, 256:512] = (value - high.astype(jnp.float32)).astype(jnp.bfloat16)
+
+        for r in range(7):
+            plain = [recv_c[pl.ds(r + 8 * c, blocks, stride=32), :] for c in range(4)]
+            moved = [pltpu.roll(x, CAP, 1) for x in plain]
+            put(r, jnp.where(low, plain[0], moved[1]), jnp.where(low, plain[2], moved[3]))
+            if r >= 1:
+                put(r + 6, jnp.where(low, moved[0], plain[1]), jnp.where(low, moved[2], plain[3]))
+
+        def select(x, carry):
+            found = jnp.dot(
+                split[...], jnp.concatenate([hot[x], hot[x]], axis=0), preferred_element_type=jnp.float32
+            )
+            match = which == seats_of(x) >> 8
+            for r in range(13):
+                piece = jnp.where(match, found[blocks * r : blocks * (r + 1)], 0.0)
+                records[r, pl.ds(x, 1), :] = jnp.sum(piece, axis=0, keepdims=True)
+            return carry
+
+        lax.fori_loop(0, 16, select, 0, unroll=2)
+
+    choose()
     loads[4].wait()
     sunlight, air, humidity, rainfall = (forcing_ref[i] for i in range(4))
     leaf, albedo, resist = (records[i] for i in range(3))
@@ -630,12 +616,10 @@
         moves = start(1 + n, 2 + n, field)
         partial = place(jnp.zeros((1, 128), jnp.float32), 0, square_of_start())
         if n:
-            linearize(*OWN)
             finish(head_moves, 4, [(head, ())])
             for region in RIM:
                 saturate(*region, keep_none)
-            for region in RIM:
-                linearize(*region)
+            linearize(False)
         finish(moves, 2 + n, field)
         for j, at in ((0, 1), (1, 3), (2, 6)):
             partial = place(partial, at, matvec(j))
@@ -683,14 +667,14 @@
     f32 = jnp.float32
     wide = (layers, ROWS, LANES)
     tile = (layers, 16, 512)
-    vmem, hbm = pl.BlockSpec(memory_space=pltpu.VMEM), pl.BlockSpec(memory_space=pltpu.HBM)
+    vmem, anywhere = pl.BlockSpec(memory_space=pltpu.VMEM), pl.BlockSpec(memory_space=pl.ANY)
     return pl.pallas_call(
         functools.partial(kernel, sizes),
         out_shape=(
             jax.ShapeDtypeStruct(head_old.shape, f32),
             jax.ShapeDtypeStruct((2, 16, 512), f32),
         ),
-        in_specs=[hbm] * 6,
+        in_specs=[anywhere] * 6,
         out_specs=(vmem, vmem),
         scratch_shapes=[
             pltpu.SMEM(soil_table.shape, f32),
@@ -700,7 +684,7 @@
             pltpu.VMEM(column_slot.shape, jnp.int32),
             pltpu.VMEM((devices, 8, 128), f32),
             pltpu.VMEM((devices * 8, 128), f32),
-            pltpu.VMEM((13 * (devices // 8), 512), jnp.bfloat16),
+            pltpu.VMEM((13 * (devices // 4), 512), jnp.bfloat16),
             pltpu.VMEM((16, 256, 512), jnp.bfloat16),
             pltpu.VMEM((13, 16, 512), f32),
             pltpu.VMEM(wide, f32),
@@ -730,9 +714,7 @@
             pltpu.SemaphoreType.DMA((2, NEWTON)),
             pltpu.SemaphoreType.DMA((2, NEWTON)),
         ],
-        compiler_params=pltpu.CompilerParams(
-            collective_id=0, has_side_effects=True, vmem_limit_bytes=40 * 1024 * 1024
-        ),
+        compiler_params=pltpu.CompilerParams(collective_id=0, has_side_effects=True),
         name="coupled_step",
     )(head_old, soil_type, soil_table, forcing, canopy, column_slot)
 

time: 79.8 us -> 68.8 us (0.86)
  Pallas kernels: 72.1 us -> 65.6 us
  local copies, waits for them, and re-layouts: 6.68 us -> 2.38 us
    pallas_call x1, Pallas kernels: 72.1 us -> 65.6 us  [shards(): pl.pallas_call(functools.partial(kernel, sizes), out_shape=(jax.ShapeDtyp...]
    unnamed x14 -> x4, local copies, waits for them, and re-layouts: 6.68 us -> 2.38 us
where the time goes in v4:
time: 68.8 us; the launch traced here: 68.6 us
  Pallas kernels  65.6 us (95%)
  local copies, waits for them, and re-layouts  2.38 us (3%)
    pallas_call x1, Pallas kernels, shards(): pl.pallas_call(functools.partial(kernel, sizes), out_shape=(jax.ShapeDtyp...  65.6 us
    unnamed x4, local copies, waits for them, and re-layouts  2.38 us

profile of v4, /device:TPU:1, one launch (start us, length us, event | category | flops | bytes accessed | tf_op | source)
XLA Modules:
  0.0 68.6 jit_solution(12534572257980874338)
XLA Ops:
  0.6 65.6 %coupled_step.1 = (f32[10,16,512]{2,1,0:T(8,128)}, f32[2,16,512]{2,1,0:T(8,128)}) custom-call(f32[10,16,512]{2,1,0:T(8,128)} %head_in.1, s32[10,16,512]{2,1,0:T(8,128)} %soil_in.1, f32[3,12]{1,0:T(4,128)} %table_in.1, f32[4,16,512]{2,1,0:T(8,128)} %forcing_in.1, f32[13,8192]{1,0:T(8,128)} %canopy_in.1, s32[16,512]{1,0:T(8,128)} %slot_in.1), custom_call_target="tpu_custom_call" | custom-call | tf_op jit(solution)/shard_map/coupled_step/pallas_call | solution.py:671
  66.2 0.0 copy-start
  66.2 1.7 %copy.10 = f32[10,16,512]{2,1,0:T(8,128)} copy(f32[10,16,512]{2,1,0:T(8,128)} %get-tuple-element.4) | data formatting | bytes 655360
  68.0 0.0 copy-done
  68.0 0.6 copy.11
Async XLA Ops:
  66.2 1.8 %copy-start = (f32[2,16,512]{2,1,0:T(8,128)S(1)}, f32[2,16,512]{2,1,0:T(8,128)}, u32[]{:S(2)}) copy-start(f32[2,16,512]{2,1,0:T(8,128)} %get-tuple-element.5) | copy-start | bytes 196612

commit v5 on v4

--- a/solution.py
+++ b/solution.py
@@ -191,10 +191,9 @@
     row = lax.broadcasted_iota(jnp.int32, (ROWS, LANES), 0)
     col = lax.broadcasted_iota(jnp.int32, (ROWS, LANES), 1)
     one, zero = jnp.float32(1.0), jnp.float32(0.0)
-    has_next_x = jnp.where(gx < size_x - 1, one, zero)
-    has_prev_x = jnp.where(gx > 0, one, zero)
-    has_next_y = jnp.where(gy < size_y - 1, one, zero)
-    has_prev_y = jnp.where(gy > 0, one, zero)
+    in_x, in_y = (gx < size_x - 1, gx > 0), (gy < size_y - 1, gy > 0)
+    has_next_x, has_prev_x = (jnp.where(there, one, zero) for there in in_x)
+    has_next_y, has_prev_y = (jnp.where(there, one, zero) for there in in_y)
     inside_x = jnp.where(
         row < 16,
         1.0,
@@ -270,14 +269,25 @@
             for turn, x in enumerate((next_x, prev_x)):
                 edge = pl.ds(8 * (1 - turn), 8)
                 plan.append(
-                    (send_y.at[side, slots, edge], recv_k.at[side, turn, slots], (x, y))
+                    (
+                        send_y.at[side, slots, edge],
+                        recv_k.at[side, turn, slots],
+                        (x, y),
+                        in_x[turn] & in_y[side],
+                        in_x[1 - turn] & in_y[1 - side],
+                    )
                 )
         for side, x in enumerate((next_x, prev_x)):
-            plan.append((send_x.at[side, slots], recv_x.at[side, slots], (x, gy)))
+            plan.append(
+                (send_x.at[side, slots], recv_x.at[side, slots], (x, gy), in_x[side], in_x[1 - side])
+            )
         for side, y in enumerate((next_y, prev_y)):
-            plan.append((send_y.at[side, slots], recv_y.at[side, slots], (gx, y)))
-        moves = [
-            pltpu.make_async_remote_copy(
+            plan.append(
+                (send_y.at[side, slots], recv_y.at[side, slots], (gx, y), in_y[side], in_y[1 - side])
+            )
+        moves = []
+        for i, (src, dst, target, sends, receives) in enumerate(plan):
+            move = pltpu.make_async_remote_copy(
                 src_ref=src,
                 dst_ref=dst,
                 send_sem=sem_e.at[0, number, i],
@@ -285,15 +295,22 @@
                 device_id=target,
                 device_id_type=MESH,
             )
-            for i, (src, dst, target) in enumerate(plan)
-        ]
-        for move in moves:
-            move.start()
+            moves.append((move, sends, receives))
+        for i in (4, 5, 0, 1, 2, 3, 6, 7):
+            move, sends, _ = moves[i]
+            pl.when(sends)(move.start)
         return moves
 
+    def await_all(moves):
+        for move, _, receives in moves:
+            pl.when(receives)(move.wait_recv)
+
+    def drain(moves):
+        for move, sends, _ in moves:
+            pl.when(sends)(move.wait_send)
+
     def finish(moves, slot, fields):
-        for move in moves[6:] + moves[:4]:
-            move.wait()
+        await_all(moves[6:] + moves[:4])
         edge = mask[:, 512:640]
         for f, (ref, index) in enumerate(fields):
             sides = [
@@ -311,13 +328,12 @@
                 right = pltpu.roll(sides[1], 128 - 4 * k, 1) if k else sides[1]
                 both = jnp.where(lane24 < 64, right, left)
                 ref[index + (k, slice(0, ROWS), slice(512, 640))] = jnp.where(edge > 0.0, both, 0.0)
-        for move in moves[4:6]:
-            move.wait()
+        await_all(moves[4:6])
         for f, (ref, index) in enumerate(fields):
             for k in range(layers):
                 rows = slice(HALO * k, HALO * (k + 1))
-                after = recv_x[1, slot + f, rows, :] * has_next_x
-                before = recv_x[0, slot + f, rows, :] * has_prev_x
+                after = jnp.where(in_x[0], recv_x[1, slot + f, rows, :], 0.0)
+                before = jnp.where(in_x[1], recv_x[0, slot + f, rows, :], 0.0)
                 ref[index + (k, slice(16, 16 + HALO), slice(0, 512))] = after
                 ref[index + (k, slice(ROWS - HALO, ROWS), slice(0, 512))] = before
 
@@ -344,6 +360,7 @@
 
     opening = [(head, ()), (soil, ())]
     moves = start(0, 0, opening)
+    started = [moves]
     others(scatter)
 
     def look_up(rows, lanes):
@@ -411,10 +428,10 @@
     def around(k):
         return jnp.minimum(k + 1, layers - 1), jnp.maximum(k - 1, 0)
 
-    def balance():
+    def balance(added):
         def layer(k, carry):
             h, kk = head[k], conduct[k]
-            total = basis[0, k, 0:16, 0:512]
+            total = basis[0, k, 0:16, 0:512] if added else 0.0
             for axis in range(2):
                 flow = 0.5 * (kk + ahead(kk, axis)) * (h - ahead(h, axis))
                 total = total + (flow - behind(flow, axis))[0:16, 0:512]
@@ -428,12 +445,11 @@
 
         lax.fori_loop(0, layers, layer, 0, unroll=2)
 
-    def linearize(flows):
+    def linearize():
         def layer(k, carry):
             scaled = mask[...] * (1.0 / SCALE)
             h, kk, dk = head[k], conduct[k], slope[k]
             diagonal = coef[0, k] - SHIFT
-            total = None
             for axis, at in ((0, 1), (1, 3)):
                 drop = h - ahead(h, axis)
                 mean = 0.5 * (kk + ahead(kk, axis))
@@ -442,25 +458,16 @@
                 diagonal = diagonal + mine - behind(other, axis)
                 coef[at, k] = other * scaled
                 coef[at + 1, k] = -behind(mine, axis) * scaled
-                if flows:
-                    flow = mean * drop
-                    net = flow - behind(flow, axis)
-                    total = net if total is None else total + net
             below, above = around(k)
             bottom, top = k == layers - 1, k == 0
             drop = h - head[below] + 1.0
             mean = 0.5 * (kk + conduct[below])
             diagonal = diagonal + jnp.where(bottom, 2.0 * dk, dk * drop + mean)
             coef[5, k] = jnp.where(bottom, 0.0, slope[below] * drop - mean) * scaled
-            if flows:
-                total = total + jnp.where(bottom, kk, mean * drop)
             drop = head[above] - h + 1.0
             mean = 0.5 * (kk + conduct[above])
             diagonal = diagonal - jnp.where(top, 0.0, dk * drop - mean)
             coef[6, k] = -jnp.where(top, 0.0, slope[above] * drop + mean) * scaled
-            if flows:
-                total = total - jnp.where(top, 0.0, mean * drop)
-                basis[0, k, 0:16, 0:512] = total[0:16, 0:512]
             coef[0, k] = diagonal * scaled
             return carry
 
@@ -468,7 +475,7 @@
 
     for region in RIM:
         saturate(*region, keep_none)
-    linearize(True)
+    balance(False)
 
     blocks = devices // 4
     low = lax.broadcasted_iota(jnp.int32, (blocks, 128), 1) < CAP
@@ -614,12 +621,15 @@
     for n in range(NEWTON):
         field = [(basis, (0,))]
         moves = start(1 + n, 2 + n, field)
+        started.append(moves)
         partial = place(jnp.zeros((1, 128), jnp.float32), 0, square_of_start())
-        if n:
+        if not n:
+            linearize()
+        else:
             finish(head_moves, 4, [(head, ())])
             for region in RIM:
                 saturate(*region, keep_none)
-            linearize(False)
+            linearize()
         finish(moves, 2 + n, field)
         for j, at in ((0, 1), (1, 3), (2, 6)):
             partial = place(partial, at, matvec(j))
@@ -647,11 +657,14 @@
         lax.fori_loop(0, layers, update, 0)
         if not last:
             head_moves = start(3, 4, [(head, ())])
+            started.append(head_moves)
             saturate(*OWN, keep_residual)
             for region in RIM:
                 saturate(*region, keep_none)
-            balance()
-
+            balance(True)
+
+    for moves in started:
+        drain(moves)
     sent = send_c.at[pl.ds(0, devices - 1), pl.ds(0, 7)]
     pltpu.make_async_copy(sent, sent, sem_c.at[0]).wait()
     for n in range(NEWTON):

time: 68.8 us -> 66.5 us (0.967)
  Pallas kernels: 65.6 us -> 63.3 us
    pallas_call x1, Pallas kernels: 65.6 us -> 63.3 us  [shards(): pl.pallas_call(functools.partial(kernel, sizes), out_shape=(jax.ShapeDtyp...]
where the time goes in v5:
time: 66.5 us; the launch traced here: 66.3 us
  Pallas kernels  63.3 us (95%)
  local copies, waits for them, and re-layouts  2.38 us (4%)
    pallas_call x1, Pallas kernels, shards(): pl.pallas_call(functools.partial(kernel, sizes), out_shape=(jax.ShapeDtyp...  63.3 us
    unnamed x4, local copies, waits for them, and re-layouts  2.38 us

profile of v5, /device:TPU:1, one launch (start us, length us, event | category | flops | bytes accessed | tf_op | source)
XLA Modules:
  0.0 66.3 jit_solution(6363193284550974959)
XLA Ops:
  0.6 63.3 %coupled_step.1 = (f32[10,16,512]{2,1,0:T(8,128)}, f32[2,16,512]{2,1,0:T(8,128)}) custom-call(f32[10,16,512]{2,1,0:T(8,128)} %head_in.1, s32[10,16,512]{2,1,0:T(8,128)} %soil_in.1, f32[3,12]{1,0:T(4,128)} %table_in.1, f32[4,16,512]{2,1,0:T(8,128)} %forcing_in.1, f32[13,8192]{1,0:T(8,128)} %canopy_in.1, s32[16,512]{1,0:T(8,128)} %slot_in.1), custom_call_target="tpu_custom_call" | custom-call | tf_op jit(solution)/shard_map/coupled_step/pallas_call | solution.py:684
  64.0 0.0 copy-start
  64.0 1.7 %copy.10 = f32[10,16,512]{2,1,0:T(8,128)} copy(f32[10,16,512]{2,1,0:T(8,128)} %get-tuple-element.4) | data formatting | bytes 655360
  65.7 0.0 copy-done
  65.7 0.6 copy.11
Async XLA Ops:
  64.0 1.8 %copy-start = (f32[2,16,512]{2,1,0:T(8,128)S(1)}, f32[2,16,512]{2,1,0:T(8,128)}, u32[]{:S(2)}) copy-start(f32[2,16,512]{2,1,0:T(8,128)} %get-tuple-element.5) | copy-start | bytes 196612

commit v6 on v5

--- a/solution.py
+++ b/solution.py
@@ -139,13 +139,11 @@
     recv_y,
     recv_k,
     part,
-    gather_x,
-    gather_y,
+    gather,
     sem_in,
     sem_c,
     sem_e,
-    sem_gx,
-    sem_gy,
+    sem_g,
 ):
     size_x, size_y = sizes
     devices = size_x * size_y
@@ -509,7 +507,7 @@
                 records[r, pl.ds(x, 1), :] = jnp.sum(piece, axis=0, keepdims=True)
             return carry
 
-        lax.fori_loop(0, 16, select, 0, unroll=2)
+        lax.fori_loop(0, 16, select, 0, unroll=16)
 
     choose()
     loads[4].wait()
@@ -595,28 +593,27 @@
         return [lax.fori_loop(0, layers, layer, jnp.zeros((8, 128), jnp.float32))]
 
     def reduce_all(n, partial):
-        def along(stage, value, gather, sem, here, size, target):
-            mine = part.at[n, stage]
-            mine[...] = value
-            gather[n, here] = value
-            for i in range(1, size):
-                pltpu.make_async_remote_copy(
-                    src_ref=mine,
-                    dst_ref=gather.at[n, here],
-                    send_sem=sem.at[0, n],
-                    recv_sem=sem.at[1, n],
-                    device_id=target(lax.rem(here + i, size)),
-                    device_id_type=MESH,
-                ).start()
-            rest = gather.at[n, pl.ds(0, size - 1)]
-            pltpu.make_async_copy(rest, rest, sem.at[1, n]).wait()
-            total = gather[n, 0]
-            for i in range(1, size):
-                total = total + gather[n, i]
-            return total
-
-        partial = along(0, partial, gather_x, sem_gx, gx, size_x, lambda d: (d, gy))
-        return along(1, partial, gather_y, sem_gy, gy, size_y, lambda d: (gx, d))
+        mine = part.at[n]
+        mine[...] = partial
+        gather[n, me] = partial
+
+        def send(x, y):
+            pltpu.make_async_remote_copy(
+                src_ref=mine,
+                dst_ref=gather.at[n, me],
+                send_sem=sem_g.at[0, n],
+                recv_sem=sem_g.at[1, n],
+                device_id=(x, y),
+                device_id_type=MESH,
+            ).start()
+
+        others(send)
+        rest = gather.at[n, pl.ds(0, devices - 1)]
+        pltpu.make_async_copy(rest, rest, sem_g.at[1, n]).wait()
+        sums = [gather[n, i] for i in range(4)]
+        for i in range(4, devices, 4):
+            sums = [a + gather[n, i + k] for k, a in enumerate(sums)]
+        return (sums[0] + sums[1]) + (sums[2] + sums[3])
 
     for n in range(NEWTON):
         field = [(basis, (0,))]
@@ -668,10 +665,8 @@
     sent = send_c.at[pl.ds(0, devices - 1), pl.ds(0, 7)]
     pltpu.make_async_copy(sent, sent, sem_c.at[0]).wait()
     for n in range(NEWTON):
-        sent = gather_x.at[n, pl.ds(0, size_x - 1)]
-        pltpu.make_async_copy(sent, sent, sem_gx.at[0, n]).wait()
-        sent = gather_y.at[n, pl.ds(0, size_y - 1)]
-        pltpu.make_async_copy(sent, sent, sem_gy.at[0, n]).wait()
+        sent = gather.at[n, pl.ds(0, devices - 1)]
+        pltpu.make_async_copy(sent, sent, sem_g.at[0, n]).wait()
 
 
 def shards(sizes, head_old, soil_type, soil_table, forcing, canopy, column_slot):
@@ -718,13 +713,11 @@
             pltpu.VMEM((2, 5, 16, 128), f32),
             pltpu.VMEM((2, 5, 16, 128), f32),
             pltpu.VMEM((2, 2, 5, 8, 128), f32),
-            pltpu.VMEM((NEWTON, 2, 1, 128), f32),
-            pltpu.VMEM((NEWTON, sizes[0], 1, 128), f32),
-            pltpu.VMEM((NEWTON, sizes[1], 1, 128), f32),
+            pltpu.VMEM((NEWTON, 1, 128), f32),
+            pltpu.VMEM((NEWTON, devices, 1, 128), f32),
             pltpu.SemaphoreType.DMA((6,)),
             pltpu.SemaphoreType.DMA((3,)),
             pltpu.SemaphoreType.DMA((2, 4, 8)),
-            pltpu.SemaphoreType.DMA((2, NEWTON)),
             pltpu.SemaphoreType.DMA((2, NEWTON)),
         ],
         compiler_params=pltpu.CompilerParams(collective_id=0, has_side_effects=True),

time: 66.5 us -> 61.6 us (0.926)
  Pallas kernels: 63.3 us -> 58.4 us
    pallas_call x1, Pallas kernels: 63.3 us -> 58.4 us  [shards(): pl.pallas_call(functools.partial(kernel, sizes), out_shape=(jax.ShapeDtyp...]
where the time goes in v6:
time: 61.6 us; the launch traced here: 61.5 us
  Pallas kernels  58.4 us (95%)
  local copies, waits for them, and re-layouts  2.38 us (4%)
  between operations  0.65 us (1%)
    pallas_call x1, Pallas kernels, shards(): pl.pallas_call(functools.partial(kernel, sizes), out_shape=(jax.ShapeDtyp...  58.4 us
    unnamed x4, local copies, waits for them, and re-layouts  2.38 us

profile of v6, /device:TPU:1, one launch (start us, length us, event | category | flops | bytes accessed | tf_op | source)
XLA Modules:
  0.0 61.5 jit_solution(5888623656470357034)
XLA Ops:
  0.6 58.4 %coupled_step.1 = (f32[10,16,512]{2,1,0:T(8,128)}, f32[2,16,512]{2,1,0:T(8,128)}) custom-call(f32[10,16,512]{2,1,0:T(8,128)} %head_in.1, s32[10,16,512]{2,1,0:T(8,128)} %soil_in.1, f32[3,12]{1,0:T(4,128)} %table_in.1, f32[4,16,512]{2,1,0:T(8,128)} %forcing_in.1, f32[13,8192]{1,0:T(8,128)} %canopy_in.1, s32[16,512]{1,0:T(8,128)} %slot_in.1), custom_call_target="tpu_custom_call" | custom-call | tf_op jit(solution)/shard_map/coupled_step/pallas_call | solution.py:679
  59.1 0.0 copy-start
  59.1 1.7 %copy.10 = f32[10,16,512]{2,1,0:T(8,128)} copy(f32[10,16,512]{2,1,0:T(8,128)} %get-tuple-element.4) | data formatting | bytes 655360
  60.8 0.0 copy-done
  60.8 0.6 %copy.11 = f32[2,16,512]{2,1,0:T(8,128)} copy(f32[2,16,512]{2,1,0:T(8,128)S(1)} %copy-done) | data formatting | bytes 131072
Async XLA Ops:
  59.1 1.8 %copy-start = (f32[2,16,512]{2,1,0:T(8,128)S(1)}, f32[2,16,512]{2,1,0:T(8,128)}, u32[]{:S(2)}) copy-start(f32[2,16,512]{2,1,0:T(8,128)} %get-tuple-element.5) | copy-start | bytes 196612

commit v7 on v6

--- a/solution.py
+++ b/solution.py
@@ -373,7 +373,7 @@
             cap[k, rows, lanes] = values[2]
             return carry
 
-        lax.fori_loop(0, layers, layer, 0)
+        lax.fori_loop(0, layers, layer, 0, unroll=2)
 
     loads[5].wait()
     look_up(*OWN)
@@ -469,7 +469,7 @@
             coef[0, k] = diagonal * scaled
             return carry
 
-        lax.fori_loop(0, layers, layer, 0)
+        lax.fori_loop(0, layers, layer, 0, unroll=2)
 
     for region in RIM:
         saturate(*region, keep_none)
@@ -583,7 +583,7 @@
             return tuple(a + b for a, b in zip(carry, sums))
 
         zeros = tuple(jnp.zeros((8, 128), jnp.float32) for _ in range(j + 2))
-        return lax.fori_loop(0, layers, layer, zeros, unroll=2)
+        return lax.fori_loop(0, layers, layer, zeros, unroll=5)
 
     def square_of_start():
         def layer(k, carry):
@@ -670,6 +670,7 @@
 
 
 def shards(sizes, head_old, soil_type, soil_table, forcing, canopy, column_slot):
+    inputs = (head_old, soil_type, soil_table, forcing, canopy, column_slot)
     layers = head_old.shape[0]
     devices = sizes[0] * sizes[1]
     f32 = jnp.float32
@@ -720,9 +721,11 @@
             pltpu.SemaphoreType.DMA((2, 4, 8)),
             pltpu.SemaphoreType.DMA((2, NEWTON)),
         ],
-        compiler_params=pltpu.CompilerParams(collective_id=0, has_side_effects=True),
+        compiler_params=pltpu.CompilerParams(
+            collective_id=0, has_side_effects=True, vmem_limit_bytes=48 * 1024 * 1024
+        ),
         name="coupled_step",
-    )(head_old, soil_type, soil_table, forcing, canopy, column_slot)
+    )(*(pltpu.with_memory_space_constraint(x, pltpu.HBM) for x in inputs))
 
 
 def solution(mesh):

time: 61.6 us -> 58.7 us (0.953)
  Pallas kernels: 58.4 us -> 56.5 us
  local copies, waits for them, and re-layouts: 2.38 us -> 1.36 us
    pallas_call x1, Pallas kernels: 58.4 us -> 56.5 us  [shards(): pl.pallas_call(functools.partial(kernel, sizes), out_shape=(jax.ShapeDtyp...]
    unnamed x4 -> x2, local copies, waits for them, and re-layouts: 2.38 us -> 1.36 us
where the time goes in v7:
time: 58.7 us; the launch traced here: 58.5 us
  Pallas kernels  56.5 us (96%)
  local copies, waits for them, and re-layouts  1.36 us (2%)
  between operations  0.64 us (1%)
    pallas_call x1, Pallas kernels, shards(): pl.pallas_call(functools.partial(kernel, sizes), out_shape=(jax.ShapeDtyp...  56.5 us
    unnamed x2, local copies, waits for them, and re-layouts  1.36 us

profile of v7, /device:TPU:1, one launch (start us, length us, event | category | flops | bytes accessed | tf_op | source)
XLA Modules:
  0.0 58.5 jit_solution(13552057524057930554)
XLA Ops:
  0.6 56.5 %coupled_step.1 = (f32[10,16,512]{2,1,0:T(8,128)S(1)}, f32[2,16,512]{2,1,0:T(8,128)S(1)}) custom-call(f32[10,16,512]{2,1,0:T(8,128)} %head_in.1, s32[10,16,512]{2,1,0:T(8,128)} %soil_in.1, f32[3,12]{1,0:T(4,128)} %table_in.1, f32[4,16,512]{2,1,0:T(8,128)} %forcing_in.1, f32[13,8192]{1,0:T(8,128)} %canopy_in.1, s32[16,512]{1,0:T(8,128)} %slot_in.1), custom_call_target="tpu_custom_call" | custom-call | tf_op jit(solution)/shard_map/coupled_step/pallas_call | solution.py:680
  57.2 0.7 %copy.10 = f32[10,16,512]{2,1,0:T(8,128)} copy(f32[10,16,512]{2,1,0:T(8,128)S(1)} %get-tuple-element.4) | data formatting | bytes 655360
  57.9 0.6 %copy.11 = f32[2,16,512]{2,1,0:T(8,128)} copy(f32[2,16,512]{2,1,0:T(8,128)S(1)} %get-tuple-element.5) | data formatting | bytes 131072

commit v8 on v7

--- a/solution.py
+++ b/solution.py
@@ -135,6 +135,8 @@
     mask,
     send_x,
     recv_x,
+    send_w,
+    recv_w,
     send_y,
     recv_y,
     recv_k,
@@ -217,6 +219,8 @@
     for side in range(2):
         for slot in range(5):
             send_x[side, slot, 24:32, :] = jnp.zeros((8, 512), jnp.float32)
+        for slot in range(2):
+            send_w[side, slot, 8:16, :] = jnp.zeros((8, 512), jnp.float32)
 
     low7 = lax.broadcasted_iota(jnp.int32, (7, 128), 1) < CAP
 
@@ -246,14 +250,43 @@
     lane24 = lax.broadcasted_iota(jnp.int32, (ROWS, 128), 1)
     early8 = lax.broadcasted_iota(jnp.int32, (8, 128), 0) < 4
 
-    def start(number, slot, fields):
+    def send_all(number, plan):
+        moves = []
+        for i, src, dst, target, sends, receives in plan:
+            move = pltpu.make_async_remote_copy(
+                src_ref=src,
+                dst_ref=dst,
+                send_sem=sem_e.at[0, number, i],
+                recv_sem=sem_e.at[1, number, i],
+                device_id=target,
+                device_id_type=MESH,
+            )
+            moves.append((move, sends, receives))
+        for move, sends, _ in moves:
+            pl.when(sends)(move.start)
+        return moves
+
+    def start_x(number, slot, fields, depth):
+        send, recv = (send_x, recv_x) if depth == HALO else (send_w, recv_w)
+        for f, (ref, index) in enumerate(fields):
+            for k in range(layers):
+                rows = slice(depth * k, depth * (k + 1))
+                send[0, slot + f, rows, :] = ref[index + (k, slice(16 - depth, 16), slice(0, 512))]
+                send[1, slot + f, rows, :] = ref[index + (k, slice(0, depth), slice(0, 512))]
+        slots = pl.ds(slot, len(fields))
+        return send_all(
+            number,
+            [
+                (side, send.at[side, slots], recv.at[side, slots], (x, gy), in_x[side], in_x[1 - side])
+                for side, x in enumerate((next_x, prev_x))
+            ],
+        )
+
+    def start_y(number, slot, fields):
         for f, (ref, index) in enumerate(fields):
             up = jnp.zeros((16, 128), jnp.float32)
             down = jnp.zeros((16, 128), jnp.float32)
             for k in range(layers):
-                rows = slice(HALO * k, HALO * (k + 1))
-                send_x[0, slot + f, rows, :] = ref[index + (k, slice(16 - HALO, 16), slice(0, 512))]
-                send_x[1, slot + f, rows, :] = ref[index + (k, slice(0, HALO), slice(0, 512))]
                 last = ref[index + (k, slice(0, 16), slice(384, 512))]
                 first = ref[index + (k, slice(0, 16), slice(0, 128))]
                 here = group16 == k
@@ -265,39 +298,32 @@
         plan = []
         for side, y in enumerate((next_y, prev_y)):
             for turn, x in enumerate((next_x, prev_x)):
-                edge = pl.ds(8 * (1 - turn), 8)
                 plan.append(
                     (
-                        send_y.at[side, slots, edge],
+                        2 + 2 * side + turn,
+                        send_y.at[side, slots, pl.ds(8 * (1 - turn), 8)],
                         recv_k.at[side, turn, slots],
                         (x, y),
                         in_x[turn] & in_y[side],
                         in_x[1 - turn] & in_y[1 - side],
                     )
                 )
-        for side, x in enumerate((next_x, prev_x)):
-            plan.append(
-                (send_x.at[side, slots], recv_x.at[side, slots], (x, gy), in_x[side], in_x[1 - side])
-            )
         for side, y in enumerate((next_y, prev_y)):
             plan.append(
-                (send_y.at[side, slots], recv_y.at[side, slots], (gx, y), in_y[side], in_y[1 - side])
+                (
+                    6 + side,
+                    send_y.at[side, slots],
+                    recv_y.at[side, slots],
+                    (gx, y),
+                    in_y[side],
+                    in_y[1 - side],
+                )
             )
-        moves = []
-        for i, (src, dst, target, sends, receives) in enumerate(plan):
-            move = pltpu.make_async_remote_copy(
-                src_ref=src,
-                dst_ref=dst,
-                send_sem=sem_e.at[0, number, i],
-                recv_sem=sem_e.at[1, number, i],
-                device_id=target,
-                device_id_type=MESH,
-            )
-            moves.append((move, sends, receives))
-        for i in (4, 5, 0, 1, 2, 3, 6, 7):
-            move, sends, _ = moves[i]
-            pl.when(sends)(move.start)
-        return moves
+        return send_all(number, plan)
+
+    def start(number, slot, fields):
+        moves = start_x(number, slot, fields, HALO)
+        return moves, start_y(number, slot, fields)
 
     def await_all(moves):
         for move, _, receives in moves:
@@ -307,8 +333,8 @@
         for move, sends, _ in moves:
             pl.when(sends)(move.wait_send)
 
-    def finish(moves, slot, fields):
-        await_all(moves[6:] + moves[:4])
+    def finish_y(moves, slot, fields):
+        await_all(moves)
         edge = mask[:, 512:640]
         for f, (ref, index) in enumerate(fields):
             sides = [
@@ -326,14 +352,21 @@
                 right = pltpu.roll(sides[1], 128 - 4 * k, 1) if k else sides[1]
                 both = jnp.where(lane24 < 64, right, left)
                 ref[index + (k, slice(0, ROWS), slice(512, 640))] = jnp.where(edge > 0.0, both, 0.0)
-        await_all(moves[4:6])
+
+    def finish_x(moves, slot, fields, depth):
+        recv = recv_x if depth == HALO else recv_w
+        await_all(moves)
         for f, (ref, index) in enumerate(fields):
             for k in range(layers):
-                rows = slice(HALO * k, HALO * (k + 1))
-                after = jnp.where(in_x[0], recv_x[1, slot + f, rows, :], 0.0)
-                before = jnp.where(in_x[1], recv_x[0, slot + f, rows, :], 0.0)
-                ref[index + (k, slice(16, 16 + HALO), slice(0, 512))] = after
-                ref[index + (k, slice(ROWS - HALO, ROWS), slice(0, 512))] = before
+                rows = slice(depth * k, depth * (k + 1))
+                after = jnp.where(in_x[0], recv[1, slot + f, rows, :], 0.0)
+                before = jnp.where(in_x[1], recv[0, slot + f, rows, :], 0.0)
+                ref[index + (k, slice(16, 16 + depth), slice(0, 512))] = after
+                ref[index + (k, slice(ROWS - depth, ROWS), slice(0, 512))] = before
+
+    def finish(moves, slot, fields):
+        finish_y(moves[1], slot, fields)
+        finish_x(moves[0], slot, fields, HALO)
 
     loads[1].wait()
     loads[2].wait()
@@ -357,8 +390,8 @@
         ).start()
 
     opening = [(head, ()), (soil, ())]
-    moves = start(0, 0, opening)
-    started = [moves]
+    near = start_x(0, 0, opening, 1), start_y(0, 0, opening)
+    started = [*near]
     others(scatter)
 
     def look_up(rows, lanes):
@@ -419,7 +452,8 @@
 
     lax.fori_loop(0, 16, spot, 0)
 
-    finish(moves, 0, opening)
+    finish_y(near[1], 0, opening)
+    finish_x(near[0], 0, opening, 1)
     for region in RIM:
         look_up(*region)
 
@@ -474,6 +508,8 @@
     for region in RIM:
         saturate(*region, keep_none)
     balance(False)
+    deep = start_x(4, 0, opening, HALO)
+    started.append(deep)
 
     blocks = devices // 4
     low = lax.broadcasted_iota(jnp.int32, (blocks, 128), 1) < CAP
@@ -592,6 +628,13 @@
 
         return [lax.fori_loop(0, layers, layer, jnp.zeros((8, 128), jnp.float32))]
 
+    def hops(step):
+        x, y = step
+        return sum((0, 1, 2, 1)[i % 4] for i in (x, x // 4, y // 2))
+
+    steps = [(x, y) for x in range(size_x) for y in range(size_y) if x or y]
+    farthest = sorted(steps, key=hops, reverse=True)
+
     def reduce_all(n, partial):
         mine = part.at[n]
         mine[...] = partial
@@ -607,7 +650,8 @@
                 device_id_type=MESH,
             ).start()
 
-        others(send)
+        for x, y in farthest:
+            send(lax.rem(gx + x, size_x), lax.rem(gy + y, size_y))
         rest = gather.at[n, pl.ds(0, devices - 1)]
         pltpu.make_async_copy(rest, rest, sem_g.at[1, n]).wait()
         sums = [gather[n, i] for i in range(4)]
@@ -618,9 +662,12 @@
     for n in range(NEWTON):
         field = [(basis, (0,))]
         moves = start(1 + n, 2 + n, field)
-        started.append(moves)
+        started.extend(moves)
         partial = place(jnp.zeros((1, 128), jnp.float32), 0, square_of_start())
         if not n:
+            finish_x(deep, 0, opening, HALO)
+            look_up(*RIM[0])
+            saturate(*RIM[0], keep_none)
             linearize()
         else:
             finish(head_moves, 4, [(head, ())])
@@ -654,7 +701,7 @@
         lax.fori_loop(0, layers, update, 0)
         if not last:
             head_moves = start(3, 4, [(head, ())])
-            started.append(head_moves)
+            started.extend(head_moves)
             saturate(*OWN, keep_residual)
             for region in RIM:
                 saturate(*region, keep_none)
@@ -711,6 +758,8 @@
             pltpu.VMEM((ROWS, LANES), f32),
             pltpu.VMEM((2, 5, 32, 512), f32),
             pltpu.VMEM((2, 5, 32, 512), f32),
+            pltpu.VMEM((2, 2, 16, 512), f32),
+            pltpu.VMEM((2, 2, 16, 512), f32),
             pltpu.VMEM((2, 5, 16, 128), f32),
             pltpu.VMEM((2, 5, 16, 128), f32),
             pltpu.VMEM((2, 2, 5, 8, 128), f32),
@@ -718,7 +767,7 @@
             pltpu.VMEM((NEWTON, devices, 1, 128), f32),
             pltpu.SemaphoreType.DMA((6,)),
             pltpu.SemaphoreType.DMA((3,)),
-            pltpu.SemaphoreType.DMA((2, 4, 8)),
+            pltpu.SemaphoreType.DMA((2, 5, 8)),
             pltpu.SemaphoreType.DMA((2, NEWTON)),
         ],
         compiler_params=pltpu.CompilerParams(

time: 58.7 us -> 56.5 us (0.963)
  Pallas kernels: 56.5 us -> 54.4 us
    pallas_call x1, Pallas kernels: 56.5 us -> 54.4 us  [shards(): pl.pallas_call(functools.partial(kernel, sizes), out_shape=(jax.ShapeDtyp...]
where the time goes in v8:
time: 56.5 us; the launch traced here: 56.4 us
  Pallas kernels  54.4 us (96%)
  local copies, waits for them, and re-layouts  1.36 us (2%)
  between operations  0.64 us (1%)
    pallas_call x1, Pallas kernels, shards(): pl.pallas_call(functools.partial(kernel, sizes), out_shape=(jax.ShapeDtyp...  54.4 us
    unnamed x2, local copies, waits for them, and re-layouts  1.36 us

profile of v8, /device:TPU:1, one launch (start us, length us, event | category | flops | bytes accessed | tf_op | source)
XLA Modules:
  0.0 56.4 jit_solution(16150779452339667630)
XLA Ops:
  0.6 54.4 %coupled_step.1 = (f32[10,16,512]{2,1,0:T(8,128)S(1)}, f32[2,16,512]{2,1,0:T(8,128)S(1)}) custom-call(f32[10,16,512]{2,1,0:T(8,128)} %head_in.1, s32[10,16,512]{2,1,0:T(8,128)} %soil_in.1, f32[3,12]{1,0:T(4,128)} %table_in.1, f32[4,16,512]{2,1,0:T(8,128)} %forcing_in.1, f32[13,8192]{1,0:T(8,128)} %canopy_in.1, s32[16,512]{1,0:T(8,128)} %slot_in.1), custom_call_target="tpu_custom_call" | custom-call | tf_op jit(solution)/shard_map/coupled_step/pallas_call | solution.py:727
  55.0 0.7 %copy.10 = f32[10,16,512]{2,1,0:T(8,128)} copy(f32[10,16,512]{2,1,0:T(8,128)S(1)} %get-tuple-element.4) | data formatting | bytes 655360
  55.8 0.6 %copy.11 = f32[2,16,512]{2,1,0:T(8,128)} copy(f32[2,16,512]{2,1,0:T(8,128)S(1)} %get-tuple-element.5) | data formatting | bytes 131072

commit v9 on v8

--- a/solution.py
+++ b/solution.py
@@ -172,7 +172,18 @@
     def wrap(value, size):
         return lax.rem(value + size, size)
 
+    def hops(step):
+        x, y = step
+        return sum((0, 1, 2, 1)[i % 4] for i in (x, x // 4, y // 2))
+
+    steps = [(x, y) for x in range(size_x) for y in range(size_y) if x or y]
+    farthest = sorted(steps, key=hops, reverse=True)
+
     def others(visit):
+        for x, y in farthest:
+            visit(lax.rem(gx + x, size_x), lax.rem(gy + y, size_y))
+
+    def ringwise(visit):
         for dy in range(1, size_y):
             visit(gx, lax.rem(gy + dy, size_y))
 
@@ -218,7 +229,7 @@
     lax.fori_loop(0, layers, clear, 0)
     for side in range(2):
         for slot in range(5):
-            send_x[side, slot, 24:32, :] = jnp.zeros((8, 512), jnp.float32)
+            send_x[side, slot, 16:32, :] = jnp.zeros((16, 512), jnp.float32)
         for slot in range(2):
             send_w[side, slot, 8:16, :] = jnp.zeros((8, 512), jnp.float32)
 
@@ -266,18 +277,29 @@
             pl.when(sends)(move.start)
         return moves
 
-    def start_x(number, slot, fields, depth):
+    def start_x(number, slot, fields, depth, skip=0):
         send, recv = (send_x, recv_x) if depth == HALO else (send_w, recv_w)
+        count = depth - skip
+        height = -(-layers * count // 8) * 8
         for f, (ref, index) in enumerate(fields):
             for k in range(layers):
-                rows = slice(depth * k, depth * (k + 1))
-                send[0, slot + f, rows, :] = ref[index + (k, slice(16 - depth, 16), slice(0, 512))]
-                send[1, slot + f, rows, :] = ref[index + (k, slice(0, depth), slice(0, 512))]
-        slots = pl.ds(slot, len(fields))
+                rows = slice(count * k, count * (k + 1))
+                send[0, slot + f, rows, :] = ref[
+                    index + (k, slice(16 - depth, 16 - skip), slice(0, 512))
+                ]
+                send[1, slot + f, rows, :] = ref[index + (k, slice(skip, depth), slice(0, 512))]
+        block = (pl.ds(slot, len(fields)), pl.ds(0, height))
         return send_all(
             number,
             [
-                (side, send.at[side, slots], recv.at[side, slots], (x, gy), in_x[side], in_x[1 - side])
+                (
+                    side,
+                    send.at[(side, *block)],
+                    recv.at[(side, *block)],
+                    (x, gy),
+                    in_x[side],
+                    in_x[1 - side],
+                )
                 for side, x in enumerate((next_x, prev_x))
             ],
         )
@@ -321,8 +343,8 @@
             )
         return send_all(number, plan)
 
-    def start(number, slot, fields):
-        moves = start_x(number, slot, fields, HALO)
+    def start(number, slot, fields, skip=0):
+        moves = start_x(number, slot, fields, HALO, skip)
         return moves, start_y(number, slot, fields)
 
     def await_all(moves):
@@ -353,20 +375,20 @@
                 both = jnp.where(lane24 < 64, right, left)
                 ref[index + (k, slice(0, ROWS), slice(512, 640))] = jnp.where(edge > 0.0, both, 0.0)
 
-    def finish_x(moves, slot, fields, depth):
+    def finish_x(moves, slot, fields, depth, skip=0):
         recv = recv_x if depth == HALO else recv_w
         await_all(moves)
         for f, (ref, index) in enumerate(fields):
             for k in range(layers):
-                rows = slice(depth * k, depth * (k + 1))
+                rows = slice((depth - skip) * k, (depth - skip) * (k + 1))
                 after = jnp.where(in_x[0], recv[1, slot + f, rows, :], 0.0)
                 before = jnp.where(in_x[1], recv[0, slot + f, rows, :], 0.0)
-                ref[index + (k, slice(16, 16 + depth), slice(0, 512))] = after
-                ref[index + (k, slice(ROWS - depth, ROWS), slice(0, 512))] = before
-
-    def finish(moves, slot, fields):
+                ref[index + (k, slice(16 + skip, 16 + depth), slice(0, 512))] = after
+                ref[index + (k, slice(ROWS - depth, ROWS - skip), slice(0, 512))] = before
+
+    def finish(moves, slot, fields, skip=0):
         finish_y(moves[1], slot, fields)
-        finish_x(moves[0], slot, fields, HALO)
+        finish_x(moves[0], slot, fields, HALO, skip)
 
     loads[1].wait()
     loads[2].wait()
@@ -392,7 +414,7 @@
     opening = [(head, ()), (soil, ())]
     near = start_x(0, 0, opening, 1), start_y(0, 0, opening)
     started = [*near]
-    others(scatter)
+    ringwise(scatter)
 
     def look_up(rows, lanes):
         def layer(k, carry):
@@ -628,13 +650,6 @@
 
         return [lax.fori_loop(0, layers, layer, jnp.zeros((8, 128), jnp.float32))]
 
-    def hops(step):
-        x, y = step
-        return sum((0, 1, 2, 1)[i % 4] for i in (x, x // 4, y // 2))
-
-    steps = [(x, y) for x in range(size_x) for y in range(size_y) if x or y]
-    farthest = sorted(steps, key=hops, reverse=True)
-
     def reduce_all(n, partial):
         mine = part.at[n]
         mine[...] = partial
@@ -650,8 +665,7 @@
                 device_id_type=MESH,
             ).start()
 
-        for x, y in farthest:
-            send(lax.rem(gx + x, size_x), lax.rem(gy + y, size_y))
+        others(send)
         rest = gather.at[n, pl.ds(0, devices - 1)]
         pltpu.make_async_copy(rest, rest, sem_g.at[1, n]).wait()
         sums = [gather[n, i] for i in range(4)]
@@ -670,7 +684,7 @@
             saturate(*RIM[0], keep_none)
             linearize()
         else:
-            finish(head_moves, 4, [(head, ())])
+            finish(head_moves, 4, [(head, ())], skip=1)
             for region in RIM:
                 saturate(*region, keep_none)
             linearize()
@@ -700,7 +714,7 @@
 
         lax.fori_loop(0, layers, update, 0)
         if not last:
-            head_moves = start(3, 4, [(head, ())])
+            head_moves = start(3, 4, [(head, ())], skip=1)
             started.extend(head_moves)
             saturate(*OWN, keep_residual)
             for region in RIM:

time: 56.5 us -> 55.7 us (0.986)
  Pallas kernels: 54.4 us -> 53.5 us
    pallas_call x1, Pallas kernels: 54.4 us -> 53.5 us  [shards(): pl.pallas_call(functools.partial(kernel, sizes), out_shape=(jax.ShapeDtyp...]
where the time goes in v9:
time: 55.7 us; the launch traced here: 55.5 us
  Pallas kernels  53.5 us (96%)
  local copies, waits for them, and re-layouts  1.36 us (2%)
  between operations  0.64 us (1%)
    pallas_call x1, Pallas kernels, shards(): pl.pallas_call(functools.partial(kernel, sizes), out_shape=(jax.ShapeDtyp...  53.5 us
    unnamed x2, local copies, waits for them, and re-layouts  1.36 us

profile of v9, /device:TPU:1, one launch (start us, length us, event | category | flops | bytes accessed | tf_op | source)
XLA Modules:
  0.0 55.5 jit_solution(4550928746614196026)
XLA Ops:
  0.6 53.5 %coupled_step.1 = (f32[10,16,512]{2,1,0:T(8,128)S(1)}, f32[2,16,512]{2,1,0:T(8,128)S(1)}) custom-call(f32[10,16,512]{2,1,0:T(8,128)} %head_in.1, s32[10,16,512]{2,1,0:T(8,128)} %soil_in.1, f32[3,12]{1,0:T(4,128)} %table_in.1, f32[4,16,512]{2,1,0:T(8,128)} %forcing_in.1, f32[13,8192]{1,0:T(8,128)} %canopy_in.1, s32[16,512]{1,0:T(8,128)} %slot_in.1), custom_call_target="tpu_custom_call" | custom-call | tf_op jit(solution)/shard_map/coupled_step/pallas_call | solution.py:741
  54.2 0.7 %copy.10 = f32[10,16,512]{2,1,0:T(8,128)} copy(f32[10,16,512]{2,1,0:T(8,128)S(1)} %get-tuple-element.4) | data formatting | bytes 655360
  54.9 0.6 %copy.11 = f32[2,16,512]{2,1,0:T(8,128)} copy(f32[2,16,512]{2,1,0:T(8,128)S(1)} %get-tuple-element.5) | data formatting | bytes 131072

commit v10 on v9

--- a/solution.py
+++ b/solution.py
@@ -157,10 +157,10 @@
         pltpu.make_async_copy(src, dst, sem_in.at[i])
         for i, (src, dst) in enumerate(
             (
-                (canopy_in, canopy_ref),
+                (canopy_in, canopy_ref.at[0]),
                 (head_in, head.at[:, 0:16, 0:512]),
                 (soil_in, soil_ref),
-                (slot_in, slot_ref),
+                (slot_in, slot_ref.at[0:16]),
                 (forcing_in, forcing_ref),
                 (table_in, table_ref),
             )
@@ -237,7 +237,7 @@
 
     def pack(q, carry):
         lanes = pl.ds(pl.multiple_of(q * 128, 128), 128)
-        first, second = canopy_ref[0:7, lanes], canopy_ref[6:13, lanes]
+        first, second = canopy_ref[0, 0:7, lanes], canopy_ref[0, 6:13, lanes]
         send_c[2 * q, 0:7] = jnp.where(low7, first, pltpu.roll(second, CAP, 1))
         send_c[2 * q + 1, 0:7] = jnp.where(low7, pltpu.roll(first, CAP, 1), second)
         return carry
@@ -593,7 +593,7 @@
     evaporation = conductance * (0.5 * jnp.exp(2.0 * (surface - air)) - humidity)
     ks_top = own(ksat, 0)
     infiltration = rainfall * ks_top / (rainfall + ks_top)
-    land = slot_ref[...] >= 0
+    land = slot_ref[0:16, :] >= 0
     evaporation = jnp.where(land, evaporation, 0.0)
     infiltration = jnp.where(land, infiltration, 0.0)
     flux_ref[0] = evaporation
@@ -750,13 +750,13 @@
             pltpu.SMEM(soil_table.shape, f32),
             pltpu.VMEM(tile, jnp.int32),
             pltpu.VMEM(forcing.shape, f32),
-            pltpu.VMEM(canopy.shape, f32),
-            pltpu.VMEM(column_slot.shape, jnp.int32),
+            pltpu.VMEM((2,) + canopy.shape, f32),
+            pltpu.VMEM((24, 512), jnp.int32),
             pltpu.VMEM((devices, 8, 128), f32),
             pltpu.VMEM((devices * 8, 128), f32),
             pltpu.VMEM((13 * (devices // 4), 512), jnp.bfloat16),
             pltpu.VMEM((16, 256, 512), jnp.bfloat16),
-            pltpu.VMEM((13, 16, 512), f32),
+            pltpu.VMEM((14, 16, 512), f32),
             pltpu.VMEM(wide, f32),
             pltpu.VMEM(wide, f32),
             pltpu.VMEM(wide, f32),
@@ -770,15 +770,15 @@
             pltpu.VMEM(tile, f32),
             pltpu.VMEM(tile, f32),
             pltpu.VMEM((ROWS, LANES), f32),
-            pltpu.VMEM((2, 5, 32, 512), f32),
-            pltpu.VMEM((2, 5, 32, 512), f32),
-            pltpu.VMEM((2, 2, 16, 512), f32),
-            pltpu.VMEM((2, 2, 16, 512), f32),
+            pltpu.VMEM((2, 6, 32, 512), f32),
+            pltpu.VMEM((2, 6, 32, 512), f32),
+            pltpu.VMEM((2, 3, 16, 512), f32),
+            pltpu.VMEM((2, 3, 16, 512), f32),
             pltpu.VMEM((2, 5, 16, 128), f32),
             pltpu.VMEM((2, 5, 16, 128), f32),
             pltpu.VMEM((2, 2, 5, 8, 128), f32),
-            pltpu.VMEM((NEWTON, 1, 128), f32),
-            pltpu.VMEM((NEWTON, devices, 1, 128), f32),
+            pltpu.VMEM((NEWTON + 8, 1, 128), f32),
+            pltpu.VMEM((NEWTON + 1, devices, 1, 128), f32),
             pltpu.SemaphoreType.DMA((6,)),
             pltpu.SemaphoreType.DMA((3,)),
             pltpu.SemaphoreType.DMA((2, 5, 8)),

time: 55.7 us -> 55.7 us (level)
  no operation moved by 1% of the time
where the time goes in v10:
time: 55.7 us; the launch traced here: 55.5 us
  Pallas kernels  53.5 us (96%)
  local copies, waits for them, and re-layouts  1.36 us (2%)
  between operations  0.64 us (1%)
    pallas_call x1, Pallas kernels, shards(): pl.pallas_call(functools.partial(kernel, sizes), out_shape=(jax.ShapeDtyp...  53.5 us
    unnamed x2, local copies, waits for them, and re-layouts  1.36 us

profile of v10, /device:TPU:1, one launch (start us, length us, event | category | flops | bytes accessed | tf_op | source)
XLA Modules:
  0.0 55.5 jit_solution(8791729172529898651)
XLA Ops:
  0.6 53.5 %coupled_step.1 = (f32[10,16,512]{2,1,0:T(8,128)S(1)}, f32[2,16,512]{2,1,0:T(8,128)S(1)}) custom-call(f32[10,16,512]{2,1,0:T(8,128)} %head_in.1, s32[10,16,512]{2,1,0:T(8,128)} %soil_in.1, f32[3,12]{1,0:T(4,128)} %table_in.1, f32[4,16,512]{2,1,0:T(8,128)} %forcing_in.1, f32[13,8192]{1,0:T(8,128)} %canopy_in.1, s32[16,512]{1,0:T(8,128)} %slot_in.1), custom_call_target="tpu_custom_call" | custom-call | tf_op jit(solution)/shard_map/coupled_step/pallas_call | solution.py:741
  54.2 0.7 %copy.10 = f32[10,16,512]{2,1,0:T(8,128)} copy(f32[10,16,512]{2,1,0:T(8,128)S(1)} %get-tuple-element.4) | data formatting | bytes 655360
  54.9 0.6 %copy.11 = f32[2,16,512]{2,1,0:T(8,128)} copy(f32[2,16,512]{2,1,0:T(8,128)S(1)} %get-tuple-element.5) | data formatting | bytes 131072

commit v11 on v10

--- a/solution.py
+++ b/solution.py
@@ -497,7 +497,7 @@
             basis[0, k, 0:16, 0:512] = total - jnp.where(k == 0, 0.0, flow)
             return carry
 
-        lax.fori_loop(0, layers, layer, 0, unroll=2)
+        lax.fori_loop(0, layers, layer, 0, unroll=5)
 
     def linearize():
         def layer(k, carry):
@@ -525,7 +525,7 @@
             coef[0, k] = diagonal * scaled
             return carry
 
-        lax.fori_loop(0, layers, layer, 0, unroll=2)
+        lax.fori_loop(0, layers, layer, 0, unroll=5)
 
     for region in RIM:
         saturate(*region, keep_none)

time: 55.7 us -> 55.2 us (level)
  no operation moved by 1% of the time
where the time goes in v11:
time: 55.2 us; the launch traced here: 55.1 us
  Pallas kernels  53.1 us (96%)
  local copies, waits for them, and re-layouts  1.36 us (2%)
  between operations  0.64 us (1%)
    pallas_call x1, Pallas kernels, shards(): pl.pallas_call(functools.partial(kernel, sizes), out_shape=(jax.ShapeDtyp...  53.1 us
    unnamed x2, local copies, waits for them, and re-layouts  1.36 us

profile of v11, /device:TPU:1, one launch (start us, length us, event | category | flops | bytes accessed | tf_op | source)
XLA Modules:
  0.0 55.1 jit_solution(8838687017968697956)
XLA Ops:
  0.6 53.1 %coupled_step.1 = (f32[10,16,512]{2,1,0:T(8,128)S(1)}, f32[2,16,512]{2,1,0:T(8,128)S(1)}) custom-call(f32[10,16,512]{2,1,0:T(8,128)} %head_in.1, s32[10,16,512]{2,1,0:T(8,128)} %soil_in.1, f32[3,12]{1,0:T(4,128)} %table_in.1, f32[4,16,512]{2,1,0:T(8,128)} %forcing_in.1, f32[13,8192]{1,0:T(8,128)} %canopy_in.1, s32[16,512]{1,0:T(8,128)} %slot_in.1), custom_call_target="tpu_custom_call" | custom-call | tf_op jit(solution)/shard_map/coupled_step/pallas_call | solution.py:741
  53.8 0.7 %copy.10 = f32[10,16,512]{2,1,0:T(8,128)} copy(f32[10,16,512]{2,1,0:T(8,128)S(1)} %get-tuple-element.4) | data formatting | bytes 655360
  54.5 0.6 %copy.11 = f32[2,16,512]{2,1,0:T(8,128)} copy(f32[2,16,512]{2,1,0:T(8,128)S(1)} %get-tuple-element.5) | data formatting | bytes 131072
